TPU v7x, 32 devices: a whole 2x2x4 slice. The times are simulated.
32 devices in a mesh: inp: 2 (over x), tm: 16 (over z, y, core).
Axes of the slice: x: 2, y: 2, z: 4, core: 2. Of those that a mesh axis runs over, the one named last changes fastest.
Arguments:
- samples: int32 [512, 524288], P('inp', 'tm'), may hold values from -8 to 7
- filter_taps: int32 [4, 2048], replicated, may hold values from -4096 to 4095
Outputs:
- visibilities: float32 [2, 1024, 512, 512], P(None, ('inp', 'tm'))
All inputs are finite; a program needn't handle non-finite values.
Results may differ from a plain program's by a relative error of at most 0.0032.
Values may be sent and summed in bfloat16 or wider, within the bound.
No kernel may reach another device: no remote copies, remote signals or barrier semaphores. Data moves between devices by JAX's collectives and lax.ppermute only.
A program may use at most 256 MiB of HBM per device.

v0:
```python
import math

import jax
import jax.numpy as jnp
import numpy as np
from jax import lax
from jax.experimental import pallas as pl
from jax.experimental.pallas import tpu as pltpu
from jax.sharding import PartitionSpec as P


INNER = 4
CHANNEL_STEPS = (8, 4, 4, 6, 6, 4)
HEAD_TERMS = 1
CHUNK = 512
Z_FIRST_GROUPS = 1
F32 = jnp.float32
BF16 = jnp.bfloat16


def next_slice(low, high, count, inner):
    def send(part, pairs):
        return lax.ppermute(part, "tm", pairs)

    via = inner // 2
    edges = range(inner, count, inner)
    detour = via > 0 and len(edges) > 0
    low = send(low, [(d, d + 1) for d in range(count - 1)])
    around = high
    if detour:
        around = send(high, [(d - 1, d + via) for d in edges])
        around = send(around, [(d + via, d) for d in edges])
    high = send(high, [(d, d + 1) for d in range(count - 1) if not detour or (d + 1) % inner])
    return low, high, around if detour else high


def turn_tables(angles, frame_len):
    turn = 2.0 * math.pi / frame_len
    return np.stack([np.cos(angles * turn), np.sin(angles * turn)], axis=-3).astype(np.float32)


def build_table(plane, coarse, fine, table, first_channel, count):
    z_count, _, places, frame_len = coarse.shape
    owners = z_count * places
    rows = count * 2 * owners
    width = min(CHUNK, frame_len)

    def channel(j, _):
        for start in range(0, frame_len, width):
            lanes = pl.ds(start, width)
            cos_c, sin_c = [
                jnp.concatenate([coarse[plane[0] ^ k, f, :, lanes] for k in range(z_count)], axis=0)
                for f in range(2)
            ]
            cos_f, sin_f = [fine[f, pl.ds(first_channel + j, 1), lanes] for f in range(2)]
            parts = (cos_c * cos_f - sin_c * sin_f, -(sin_c * cos_f + cos_c * sin_f))
            for p, exact in enumerate(parts):
                row = pl.multiple_of((2 * j + p) * owners, owners)
                rounded = exact.astype(BF16)
                table[pl.ds(row, owners), lanes] = rounded
                if table.shape[0] == 2 * rows:
                    rest = (exact - rounded.astype(F32)).astype(BF16)
                    table[pl.ds(rows + row, owners), lanes] = rest
        return 0

    lax.fori_loop(0, count, channel, 0)


def transform(frame, table, spread, offset, period, parts):
    contract = (((1,), (1,)), ((), ()))
    spectra = lax.dot_general(table[...], frame, contract, preferred_element_type=F32)
    lanes, length, width = spread.shape
    owners = length // period
    rows = owners * parts
    if spectra.shape[0] == 2 * rows:
        spectra = spectra[:rows] + spectra[rows:]
    for part in range(parts):
        piece = spectra[part * owners : (part + 1) * owners]
        for lane in range(lanes):
            where = pl.ds(offset + 8 * part, owners, stride=period)
            spread[lane, where, :] = piece[:, lane * width : (lane + 1) * width]


def flush(spread, outs):
    lanes, _, width = spread.shape
    views = outs if len(outs) > 1 else [outs[0].at[:, k] for k in range(outs[0].shape[1])]
    places, span, _ = views[0].shape

    def place(i, _):
        for lane in range(lanes):
            for k, view in enumerate(views):
                part = spread[lane, pl.ds(pl.multiple_of((k * places + i) * span, span), span), :]
                view[i, :, lane * width : (lane + 1) * width] = part.astype(BF16)
        return 0

    lax.fori_loop(0, places, place, 0)


def tail_kernel(samples, low, high):
    half = low.shape[0]
    low[...] = samples[:half].astype(F32).astype(BF16)
    high[...] = samples[half:].astype(F32).astype(BF16)


def filter_kernel(plane, *refs, history, count, keep):
    old, refs = refs[:history], refs[history:]
    samples, taps, coarse, fine, filtered, *outs, table, spread, recent, current = refs
    step = pl.program_id(0)
    inputs, frame_len = samples.shape
    width = min(256, frame_len)
    depth = min(16, inputs)

    @pl.when(step == 0)
    def _():
        build_table(plane, coarse, fine, table, 0, count)
        for k in range(keep):
            if history == keep:
                recent[k] = old[k][...].astype(F32).astype(BF16)
                continue
            low, high, around = old[3 * k : 3 * k + 3]
            recent[k, : inputs // 2] = low[...]

            @pl.when(plane[1] == 0)
            def _():
                recent[k, inputs // 2 :] = around[...]

            @pl.when(plane[1] != 0)
            def _():
                recent[k, inputs // 2 :] = high[...]

    slots = [lax.rem(step + k, keep) for k in range(keep)]

    def columns(i, _):
        lanes = pl.ds(pl.multiple_of(i * width, width), width)
        weights = taps[:, lanes].astype(F32) * (1.0 / 16384.0)
        weights = [jnp.broadcast_to(weights[k : k + 1], (depth, width)) for k in range(keep + 1)]
        for start in range(0, inputs, depth):
            here = pl.ds(start, depth)
            newest = samples[here, lanes].astype(F32)
            total = weights[0] * recent[slots[0], here, lanes].astype(F32)
            for k in range(1, keep):
                total = total + weights[k] * recent[slots[k], here, lanes].astype(F32)
            total = total + weights[keep] * newest
            current[here, lanes] = total.astype(BF16)
            recent[slots[0], here, lanes] = newest.astype(BF16)
        return 0

    lax.fori_loop(0, frame_len // width, columns, 0)
    filtered[0] = current[...]
    transform(current[...], table, spread, step, 16 * count, 2 * count)

    @pl.when(step == pl.num_programs(0) - 1)
    def _():
        flush(spread, outs)


def transform_kernel(plane, early, late, coarse, fine, *rest, first_channel, count):
    *outs, table, spread = rest
    step = pl.program_id(0)

    @pl.when(step == 0)
    def _():
        build_table(plane, coarse, fine, table, first_channel, count)

    for half, frame in enumerate((early, late)):
        transform(frame[0], table, spread, 16 * count * half + step, 32 * count, 2 * count)

    @pl.when(step == pl.num_programs(0) - 1)
    def _():
        flush(spread, outs)


def correlate_kernel(*refs, sources, inp_count, scale):
    out = refs[-1]
    parts = []
    for p in range(2):
        pieces = [[] for _ in range(inp_count)]
        for ref in refs[:sources]:
            part = ref[...].astype(F32)[..., 8 * p : 8 * p + 8, :]
            part = part.reshape(inp_count, -1, part.shape[-1])
            for i in range(inp_count):
                pieces[i].append(part[i])
        joined = [jnp.concatenate(each, axis=0) if len(each) > 1 else each[0] for each in pieces]
        whole = jnp.concatenate(joined, axis=1) if inp_count > 1 else joined[0]
        parts.append(whole.astype(BF16))
    real, imag = parts
    real_t, imag_t = real.T, imag.T

    def product(left, right):
        return lax.dot_general(left, right, (((1,), (0,)), ((), ())), preferred_element_type=F32)

    out[0, 0] = (product(real_t, real) + product(imag_t, imag)) * scale
    out[1, 0] = (product(imag_t, real) - product(real_t, imag)) * scale


def on_device(samples, filter_taps):
    local_inputs = samples.shape[0]
    tap_count, frame_len = filter_taps.shape
    steps = samples.shape[1] // frame_len
    channels = frame_len // 2
    inp_count = lax.axis_size("inp")
    tm_count = lax.axis_size("tm")
    inner = math.gcd(INNER, tm_count)
    z_count = tm_count // inner
    places = inp_count * inner
    owners = z_count * places
    all_inputs = local_inputs * inp_count
    chan_dev = channels // owners
    total_spectra = steps * tm_count
    keep = tap_count - 1
    half = steps // 2
    lane_width = min(128, local_inputs)
    lanes = local_inputs // lane_width

    owner_ids = np.arange(owners).reshape(inp_count, z_count, inner).transpose(1, 0, 2).reshape(z_count, places)
    points = np.arange(frame_len)
    coarse = jnp.asarray(turn_tables(owner_ids[..., None] * chan_dev * points % frame_len, frame_len))
    fine = jnp.asarray(turn_tables(np.arange(chan_dev)[:, None] * points % frame_len, frame_len))
    plane = jnp.stack([lax.axis_index("tm") // inner, lax.axis_index("tm") % inner]).astype(jnp.int32)

    head = min(CHANNEL_STEPS[0], chan_dev)
    bounds = [0]
    for number in range(chan_dev):
        if bounds[-1] < chan_dev:
            bounds.append(min(chan_dev, bounds[-1] + CHANNEL_STEPS[min(number, len(CHANNEL_STEPS) - 1)]))
    groups = list(zip(bounds[:-1], bounds[1:]))

    tail_shape = jax.ShapeDtypeStruct((local_inputs // 2, keep * frame_len), BF16)
    tail_spec = pl.BlockSpec((local_inputs // 2, frame_len), lambda s: (0, s))
    tail = pl.pallas_call(
        tail_kernel,
        grid=(keep,),
        in_specs=[pl.BlockSpec((local_inputs, frame_len), lambda s: (0, steps - keep + s))],
        out_specs=[tail_spec, tail_spec],
        out_shape=[tail_shape, tail_shape],
        name="tail",
    )(samples)
    halo = next_slice(*tail, tm_count, inner)
    once = pl.Buffered(1)

    def whole(*shape):
        return pl.BlockSpec(shape, lambda s: (0,) * len(shape), pipeline_mode=once)

    def scratch(count, halves, terms):
        rows = 2 * count * owners
        return [
            pltpu.VMEM((terms * rows, frame_len), BF16),
            pltpu.VMEM((lanes, rows * 8 * halves, lane_width), F32),
        ]

    scalar = pl.BlockSpec(memory_space=pltpu.SMEM)
    tables = [whole(*coarse.shape), whole(*fine.shape)]
    frame_spec = pl.BlockSpec((1, local_inputs, frame_len), lambda s: (s, 0, 0))

    def at_frame(index, count=local_inputs):
        return pl.BlockSpec((count, frame_len), lambda s: (0, index), pipeline_mode=once)

    def filtered_half(first, history, history_specs):
        piece = jax.ShapeDtypeStruct((places, 16 * head, local_inputs), BF16)
        return pl.pallas_call(
            lambda *refs: filter_kernel(*refs, history=len(history), count=head, keep=keep),
            grid=(half,),
            in_specs=[
                scalar,
                *history_specs,
                pl.BlockSpec((local_inputs, frame_len), lambda s: (0, first + s)),
                whole(tap_count, frame_len),
                *tables,
            ],
            out_specs=[frame_spec] + [whole(*piece.shape)] * z_count,
            out_shape=[jax.ShapeDtypeStruct((half, local_inputs, frame_len), BF16)] + [piece] * z_count,
            scratch_shapes=[
                *scratch(head, 1, HEAD_TERMS),
                pltpu.VMEM((keep, local_inputs, frame_len), BF16),
                pltpu.VMEM((local_inputs, frame_len), BF16),
            ],
            name="filter_transform",
        )(plane, *history, samples, filter_taps, coarse, fine)

    def across(value, k):
        pairs = [(z * inner + i, (z ^ k) * inner + i) for z in range(z_count) for i in range(inner)]
        return lax.ppermute(value, "tm", pairs)

    plane_groups = [
        [x * tm_count + z * inner + i for x in range(inp_count) for i in range(inner)] for z in range(z_count)
    ]

    def within(value):
        return lax.all_to_all(
            value, ("inp", "tm"), split_axis=0, concat_axis=0, axis_index_groups=plane_groups, tiled=True
        )

    def z_stage(pieces):
        return [pieces[0]] + [across(pieces[k], k) for k in range(1, z_count)]

    late, *late_pieces = filtered_half(half, [samples] * keep, [at_frame(half - keep + k) for k in range(keep)])
    z_first = z_stage(late_pieces)
    halo_specs = [at_frame(k, local_inputs // 2) for k in range(keep) for _ in range(3)]
    early, *early_pieces = filtered_half(0, list(halo) * keep, halo_specs)
    z_first += z_stage(early_pieces)

    arrived = {}
    z_first_groups = [(0, head, 1, 2 * z_count, 0)]
    for number, (first, last) in enumerate(groups[1:], 2):
        count = last - first
        goes_first = number < 2 + Z_FIRST_GROUPS and 2 * count == head
        if goes_first:
            outs = [jax.ShapeDtypeStruct((places, 32 * count, local_inputs), BF16)] * z_count
        else:
            outs = [jax.ShapeDtypeStruct((places, z_count, 32 * count, local_inputs), BF16)]
        call = pl.pallas_call(
            lambda *refs, first=first, count=count: transform_kernel(*refs, first_channel=first, count=count),
            grid=(half,),
            in_specs=[scalar, frame_spec, frame_spec, *tables],
            out_specs=[whole(*out.shape) for out in outs],
            out_shape=outs,
            scratch_shapes=scratch(count, 2, 2),
            name="transform",
        )
        value = call(plane, early, late, coarse, fine)
        if goes_first:
            z_first_groups.append((first, last, 2, z_count, len(z_first) // z_count))
            z_first += z_stage(value)
        else:
            value = within(value[0])
            moved = [value[:, 0]] + [across(value[:, k], k) for k in range(1, z_count)]
            arrived[first, last] = [
                (each.reshape(places, 1, 2, 16 * count, local_inputs), 1, 0) for each in moved
            ]
    value = within(jnp.stack(z_first, axis=1))
    for first, last, halves, lead, index in z_first_groups:
        shape = (places, len(z_first), halves, value.shape[2] // halves, local_inputs)
        arrived[first, last] = [(value.reshape(shape), lead, index)]

    ready = sorted(arrived)
    plane_first = ready[len(z_first_groups) :]
    order = plane_first[:-2] + ready[: len(z_first_groups)] + plane_first[-2:]
    result = None
    for first, last in order:
        operands, specs = [], []
        block_inp = inp_count
        for value, lead, index in arrived[first, last]:
            if local_inputs % 128:
                block_inp = 1
                value = value.reshape(inp_count, inner, *value.shape[1:])
                value = jnp.transpose(value, (1, 2, 3, 4, 0, 5))
                value = value.reshape(*value.shape[:4], all_inputs)
            operands.append(value)
            block = (value.shape[0], lead, value.shape[2], 16, value.shape[4])
            specs.append(pl.BlockSpec(block, lambda c, index=index: (0, index, 0, c, 0)))
        sources = len(operands)
        if result is not None:
            operands.append(result)
            specs.append(pl.BlockSpec(memory_space=pl.ANY))
        result = pl.pallas_call(
            lambda *refs, block_inp=block_inp, sources=sources: correlate_kernel(
                *refs, sources=sources, inp_count=block_inp, scale=1.0 / (frame_len * total_spectra)
            ),
            grid=(last - first,),
            in_specs=specs,
            out_specs=pl.BlockSpec(
                (2, 1, all_inputs, all_inputs), lambda c, first=first: (0, first + c, 0, 0)
            ),
            out_shape=jax.ShapeDtypeStruct((2, chan_dev, all_inputs, all_inputs), F32),
            input_output_aliases={} if result is None else {sources: 0},
            name="correlate",
        )(*operands)
    return result


def solution(mesh):
    placed = (P("inp", "tm"), P())
    return jax.shard_map(
        on_device,
        mesh=mesh,
        in_specs=placed,
        out_specs=P(None, ("inp", "tm"), None, None),
        check_vma=False,
    )
```

profile of v0, /device:TPU:0, one launch (start us, length us, event | category | flops | bytes accessed | tf_op | source)
XLA Modules:
  0.0 551.6 jit_solution(14611564466375158258)
XLA Ops:
  0.0 5.3 tail.1
  9.6 4.5 collective-permute-start
  16.6 24.1 %filter_transform.3 = (bf16[8,256,2048]{2,1,0:T(8,128)(2,1)}, bf16[8,128,256]{2,1,0:T(8,128)(2,1)}, bf16[8,128,256]{2,1,0:T(8,128)(2,1)}, bf16[8,128,256]{2,1,0:T(8,128)(2,1)}, bf16[8,128,256]{2,1,0:T(8,128)(2,1)}) custom-call(s32[2]{0:T(128)} %pad_add_fusion.refs_0_, s32[256,32768]{1,0:T(8,128)} %refs_4_.6, s32[256,32768]{1,0:T(8,128)} %refs_4_.6, ...), custom_call_target="tpu_custom_call" | custom-call | tf_op jit(solution)/shard_map/filter_transform/pallas_call | solution.py:260
  42.4 23.7 %filter_transform.2 = (bf16[8,256,2048]{2,1,0:T(8,128)(2,1)}, bf16[8,128,256]{2,1,0:T(8,128)(2,1)}, bf16[8,128,256]{2,1,0:T(8,128)(2,1)}, bf16[8,128,256]{2,1,0:T(8,128)(2,1)}, bf16[8,128,256]{2,1,0:T(8,128)(2,1)}) custom-call(s32[2]{0:T(128)} %pad_add_fusion.refs_0_, bf16[128,6144]{1,0:T(8,128)(2,1)} %copy-done.1, bf16[128,6144]{1,0:T(8,128)(2,1)} %copy-done, ...), custom_call_target="tpu_custom_call" | custom-call | tf_op jit(solution)/shard_map/filter_transform/pallas_call | solution.py:260
  66.1 18.2 %transform.9 = bf16[8,4,128,256]{3,2,1,0:T(8,128)(2,1)} custom-call(s32[2]{0:T(128)} %pad_add_fusion.refs_0_, bf16[8,256,2048]{2,1,0:T(8,128)(2,1)} %get-tuple-element.23.refs_1_, bf16[8,256,2048]{2,1,0:T(8,128)(2,1)} %get-tuple-element.24.refs_2_, f32[4,2,8,2048]{3,2,1,0:T(8,128)} %constant.34.clone.refs_12_.refs_6_.refs_3_, ...), custom_call_target="tpu_custom_call" | custom-call | tf_op jit(solution)/shard_map/transform/pallas_call | solution.py:320
  84.3 17.2 %all-to-all-start.4 = ((bf16[8,4,128,256]{3,2,1,0:T(8,128)(2,1)}), bf16[8,4,128,256]{3,2,1,0:T(8,128)(2,1)S(1)}, u32[]{:S(2)}, u32[]{:S(2)}) async-start(bf16[8,4,128,256]{3,2,1,0:T(8,128)(2,1)} %transform.9), calls=%async_computation.4 | async-start | bytes 4194304 | tf_op jit(solution)/shard_map/all_to_all | solution.py:289
  101.5 18.2 %transform.5 = bf16[8,4,128,256]{3,2,1,0:T(8,128)(2,1)} custom-call(s32[2]{0:T(128)} %pad_add_fusion.refs_0_, bf16[8,256,2048]{2,1,0:T(8,128)(2,1)} %get-tuple-element.23.refs_1_, bf16[8,256,2048]{2,1,0:T(8,128)(2,1)} %get-tuple-element.24.refs_2_, f32[4,2,8,2048]{3,2,1,0:T(8,128)} %constant.34.clone.refs_12_.refs_6_.refs_3_, ...), custom_call_target="tpu_custom_call" | custom-call | tf_op jit(solution)/shard_map/transform/pallas_call | solution.py:320
  119.7 7.5 %all-to-all-done.4 = bf16[8,4,128,256]{3,2,1,0:T(8,128)(2,1)S(1)} async-done(((bf16[8,4,128,256]{3,2,1,0:T(8,128)(2,1)}), bf16[8,4,128,256]{3,2,1,0:T(8,128)(2,1)S(1)}, u32[]{:S(2)}, u32[]{:S(2)}) %all-to-all-start.4) | async-done | bytes 2097184 | tf_op jit(solution)/shard_map/all_to_all | solution.py:289
  128.6 3.6 all-to-all-start
  132.2 25.1 %transform.6 = bf16[8,4,192,256]{3,2,1,0:T(8,128)(2,1)} custom-call(s32[2]{0:T(128)} %pad_add_fusion.refs_0_, bf16[8,256,2048]{2,1,0:T(8,128)(2,1)} %get-tuple-element.23.refs_1_, bf16[8,256,2048]{2,1,0:T(8,128)(2,1)} %get-tuple-element.24.refs_2_, f32[4,2,8,2048]{3,2,1,0:T(8,128)} %constant.34.clone.refs_12_.refs_6_.refs_3_, ...), custom_call_target="tpu_custom_call" | custom-call | tf_op jit(solution)/shard_map/transform/pallas_call | solution.py:320
  159.2 3.6 all-to-all-start.1
  162.9 9.0 %collective-permute-start.10 = (bf16[8,128,256]{2,1,0:T(8,128)(2,1)}, bf16[8,128,256]{2,1,0:T(8,128)(2,1)}, u32[]{:S(2)}, u32[]{:S(2)}) collective-permute-start(bf16[8,128,256]{2,1,0:T(8,128)(2,1)} %get-tuple-element.26), channel_id=1, source_target_pairs={{0,4},{1,5},{2,6},{3,7},{4,0},{5,1},{6,2},{7,3},{8,12},{9,13},{10,... | collective-permute-start | bytes 1572872 | tf_op jit(solution)/shard_map/ppermute | solution.py:282
  176.4 25.1 %transform.8 = bf16[8,4,192,256]{3,2,1,0:T(8,128)(2,1)} custom-call(s32[2]{0:T(128)} %pad_add_fusion.refs_0_, bf16[8,256,2048]{2,1,0:T(8,128)(2,1)} %get-tuple-element.23.refs_1_, bf16[8,256,2048]{2,1,0:T(8,128)(2,1)} %get-tuple-element.24.refs_2_, f32[4,2,8,2048]{3,2,1,0:T(8,128)} %constant.34.clone.refs_12_.refs_6_.refs_3_, ...), custom_call_target="tpu_custom_call" | custom-call | tf_op jit(solution)/shard_map/transform/pallas_call | solution.py:320
  201.5 4.7 all-to-all-start.3
  208.1 7.2 %collective-permute-start.13 = (bf16[8,128,256]{2,1,0:T(8,128)(2,1)}, bf16[8,128,256]{2,1,0:T(8,128)(2,1)}, u32[]{:S(2)}, u32[]{:S(2)}) collective-permute-start(bf16[8,128,256]{2,1,0:T(8,128)(2,1)} %get-tuple-element.30), channel_id=1, source_target_pairs={{0,4},{1,5},{2,6},{3,7},{4,0},{5,1},{6,2},{7,3},{8,12},{9,13},{10,... | collective-permute-start | bytes 1572872 | tf_op jit(solution)/shard_map/ppermute | solution.py:282
  221.8 18.3 %transform.7 = (bf16[8,128,256]{2,1,0:T(8,128)(2,1)}, bf16[8,128,256]{2,1,0:T(8,128)(2,1)}, bf16[8,128,256]{2,1,0:T(8,128)(2,1)}, bf16[8,128,256]{2,1,0:T(8,128)(2,1)}) custom-call(s32[2]{0:T(128)} %pad_add_fusion.refs_0_, bf16[8,256,2048]{2,1,0:T(8,128)(2,1)} %get-tuple-element.23.refs_1_, bf16[8,256,2048]{2,1,0:T(8,128)(2,1)} %get-tuple-element.24.refs_2_, ...), custom_call_target="tpu_custom_call" | custom-call | tf_op jit(solution)/shard_map/transform/pallas_call | solution.py:320
  251.2 5.7 %collective-permute-done.15 = bf16[8,128,256]{2,1,0:T(8,128)(2,1)S(1)} collective-permute-done((bf16[8,128,256]{2,1,0:T(8,128)(2,1)}, bf16[8,128,256]{2,1,0:T(8,128)(2,1)S(1)}, u32[]{:S(2)}, u32[]{:S(2)}) %collective-permute-start.15) | collective-permute-done | bytes 524320 | tf_op jit(solution)/shard_map/ppermute | solution.py:282
  259.6 6.9 %collective-permute-done.16 = bf16[8,128,256]{2,1,0:T(8,128)(2,1)S(1)} collective-permute-done((bf16[8,128,256]{2,1,0:T(8,128)(2,1)}, bf16[8,128,256]{2,1,0:T(8,128)(2,1)S(1)}, u32[]{:S(2)}, u32[]{:S(2)}) %collective-permute-start.16) | collective-permute-done | bytes 524320 | tf_op jit(solution)/shard_map/ppermute | solution.py:282
  267.4 33.2 %collective-permute-done.17 = bf16[8,128,256]{2,1,0:T(8,128)(2,1)S(1)} collective-permute-done((bf16[8,128,256]{2,1,0:T(8,128)(2,1)}, bf16[8,128,256]{2,1,0:T(8,128)(2,1)S(1)}, u32[]{:S(2)}, u32[]{:S(2)}) %collective-permute-start.17) | collective-permute-done | bytes 524320 | tf_op jit(solution)/shard_map/ppermute | solution.py:282
  302.3 4.8 all-to-all-start.2
  312.0 8.9 %collective-permute-start.23 = (bf16[8,128,256]{2,1,0:T(8,128)(2,1)S(1)}, bf16[8,128,256]{2,1,0:T(8,128)(2,1)S(1)}, u32[]{:S(2)}, u32[]{:S(2)}) collective-permute-start(bf16[8,128,256]{2,1,0:T(8,128)(2,1)S(1)} %get-tuple-element.46), channel_id=1, source_target_pairs={{0,8},{1,9},{2,10},{3,11},{4,12},{5,13},{6,14},{7,15},{8,0},{9,1},... | collective-permute-start | bytes 1572872 | tf_op jit(solution)/shard_map/ppermute | solution.py:282
  328.9 20.3 %collective-permute-start.19 = (bf16[8,192,256]{2,1,0:T(8,128)(2,1)S(1)}, bf16[8,192,256]{2,1,0:T(8,128)(2,1)S(1)}, u32[]{:S(2)}, u32[]{:S(2)}) collective-permute-start(bf16[8,192,256]{2,1,0:T(8,128)(2,1)S(1)} %get-tuple-element.39), channel_id=1, source_target_pairs={{0,4},{1,5},{2,6},{3,7},{4,0},{5,1},{6,2},{7,3},{8,12},{9,13},{10,... | collective-permute-start | bytes 2359304 | tf_op jit(solution)/shard_map/ppermute | solution.py:282
  349.2 43.8 %collective-permute-done.23 = bf16[8,128,256]{2,1,0:T(8,128)(2,1)S(1)} collective-permute-done((bf16[8,128,256]{2,1,0:T(8,128)(2,1)S(1)}, bf16[8,128,256]{2,1,0:T(8,128)(2,1)S(1)}, u32[]{:S(2)}, u32[]{:S(2)}) %collective-permute-start.23) | collective-permute-done | bytes 524320 | tf_op jit(solution)/shard_map/ppermute | solution.py:282
  395.6 48.6 %collective-permute-start.7 = (bf16[8,192,256]{2,1,0:T(8,128)(2,1)}, bf16[8,192,256]{2,1,0:T(8,128)(2,1)S(1)}, u32[]{:S(2)}, u32[]{:S(2)}) collective-permute-start(bf16[8,192,256]{2,1,0:T(8,128)(2,1)} %get-tuple-element.43), channel_id=1, source_target_pairs={{0,4},{1,5},{2,6},{3,7},{4,0},{5,1},{6,2},{7,3},{8,12},{9,13},{10,... | collective-permute-start | bytes 2359304 | tf_op jit(solution)/shard_map/ppermute | solution.py:282
  445.6 14.8 %collective-permute-done.20 = bf16[8,192,256]{2,1,0:T(8,128)(2,1)S(1)} collective-permute-done((bf16[8,192,256]{2,1,0:T(8,128)(2,1)S(1)}, bf16[8,192,256]{2,1,0:T(8,128)(2,1)S(1)}, u32[]{:S(2)}, u32[]{:S(2)}) %collective-permute-start.20) | collective-permute-done | bytes 786464 | tf_op jit(solution)/shard_map/ppermute | solution.py:282
  463.0 37.4 %collective-permute-start.4 = (bf16[8,128,256]{2,1,0:T(8,128)(2,1)}, bf16[8,128,256]{2,1,0:T(8,128)(2,1)}, u32[]{:S(2)}, u32[]{:S(2)}) collective-permute-start(bf16[8,128,256]{2,1,0:T(8,128)(2,1)} %get-tuple-element.51), channel_id=1, source_target_pairs={{0,4},{1,5},{2,6},{3,7},{4,0},{5,1},{6,2},{7,3},{8,12},{9,13},{10,... | collective-permute-start | bytes 1572872 | tf_op jit(solution)/shard_map/ppermute | solution.py:282
  500.4 6.8 %correlate.6.refs_4_ = f32[2,32,512,512]{3,2,1,0:T(8,128)} custom-call(bf16[8,1,2,64,256]{4,3,2,1,0:T(8,128)(2,1)} %bitcast.70, bf16[8,1,2,64,256]{4,3,2,1,0:T(8,128)(2,1)} %bitcast.80, bf16[8,1,2,64,256]{4,3,2,1,0:T(8,128)(2,1)} %bitcast.79, bf16[8,1,2,64,256]{4,3,2,1,0:T(8,128)(2,1)} %bitcast.78), custom_call_target="tpu_custom_call" | custom-call | tf_op jit(solution)/shard_map/correlate/pallas_call | solution.py:355
  507.2 9.4 %correlate.7.refs_1_ = f32[2,32,512,512]{3,2,1,0:T(8,128)} custom-call(bf16[8,1,2,96,256]{4,3,2,1,0:T(8,128)(2,1)} %bitcast.69, bf16[8,1,2,96,256]{4,3,2,1,0:T(8,128)(2,1)} %bitcast.77, bf16[8,1,2,96,256]{4,3,2,1,0:T(8,128)(2,1)} %bitcast.74, bf16[8,1,2,96,256]{4,3,2,1,0:T(8,128)(2,1)} %bitcast.72, ...), custom_call_target="tpu_custom_call", output_to_operand_aliasing={{}: (4, {})} | custom-call | tf_op jit(solution)/shard_map/correlate/pallas_call | solution.py:355
  516.6 11.2 %correlate.8.refs_1_ = f32[2,32,512,512]{3,2,1,0:T(8,128)} custom-call(bf16[8,12,1,128,256]{4,3,2,1,0:T(8,128)(2,1)} %bitcast.29.refs_0_, f32[2,32,512,512]{3,2,1,0:T(8,128)} %correlate.7.refs_1_), custom_call_target="tpu_custom_call", output_to_operand_aliasing={{}: (1, {})} | custom-call | tf_op jit(solution)/shard_map/correlate/pallas_call | solution.py:355
  527.7 6.6 %correlate.9.refs_4_ = f32[2,32,512,512]{3,2,1,0:T(8,128)} custom-call(bf16[8,12,2,64,256]{4,3,2,1,0:T(8,128)(2,1)} %bitcast.28.refs_0_, f32[2,32,512,512]{3,2,1,0:T(8,128)} %correlate.8.refs_1_), custom_call_target="tpu_custom_call", output_to_operand_aliasing={{}: (1, {})} | custom-call | tf_op jit(solution)/shard_map/correlate/pallas_call | solution.py:355
  535.5 9.3 %correlate.10.refs_4_ = f32[2,32,512,512]{3,2,1,0:T(8,128)} custom-call(bf16[8,1,2,96,256]{4,3,2,1,0:T(8,128)(2,1)} %bitcast.68, bf16[8,1,2,96,256]{4,3,2,1,0:T(8,128)(2,1)} %bitcast.76, bf16[8,1,2,96,256]{4,3,2,1,0:T(8,128)(2,1)} %bitcast.75, bf16[8,1,2,96,256]{4,3,2,1,0:T(8,128)(2,1)} %bitcast.73, ...), custom_call_target="tpu_custom_call", output_to_operand_aliasing={{}: (4, {})} | custom-call | tf_op jit(solution)/shard_map/correlate/pallas_call | solution.py:355
  544.8 6.8 %correlate.11 = f32[2,32,512,512]{3,2,1,0:T(8,128)} custom-call(bf16[8,1,2,64,256]{4,3,2,1,0:T(8,128)(2,1)} %bitcast.71, bf16[8,1,2,64,256]{4,3,2,1,0:T(8,128)(2,1)} %bitcast.4.refs_1_, bf16[8,1,2,64,256]{4,3,2,1,0:T(8,128)(2,1)} %bitcast.6.refs_2_, bf16[8,1,2,64,256]{4,3,2,1,0:T(8,128)(2,1)} %bitcast.8.refs_3_, ...), custom_call_target="tpu_custom_call", output_to_operand_aliasing={{}: (4, {})} | custom-call | tf_op jit(solution)/shard_map/correlate/pallas_call | solution.py:355
  (87 shorter events, 61.7 us)
Async XLA Ops:
  5.3 8.8 %collective-permute-start.2 = (bf16[128,6144]{1,0:T(8,128)(2,1)}, bf16[128,6144]{1,0:T(8,128)(2,1)}, u32[]{:S(2)}, u32[]{:S(2)}) collective-permute-start(bf16[128,6144]{1,0:T(8,128)(2,1)} %get-tuple-element.22), channel_id=1, source_target_pairs={{3,6},{7,10},{11,14},{19,22},{23,26},{27,30}} | collective-permute-start | bytes 4718600 | tf_op jit(solution)/shard_map/ppermute | solution.py:23
  7.1 33.7 %collective-permute-start.1 = (bf16[128,6144]{1,0:T(8,128)(2,1)}, bf16[128,6144]{1,0:T(8,128)(2,1)S(1)}, u32[]{:S(2)}, u32[]{:S(2)}) collective-permute-start(bf16[128,6144]{1,0:T(8,128)(2,1)} %get-tuple-element.22), channel_id=1, source_target_pairs={{0,1},{1,2},{2,3},{4,5},{5,6},{6,7},{8,9},{9,10},{10,11},{12,13},{... | collective-permute-start | bytes 4718600 | tf_op jit(solution)/shard_map/ppermute | solution.py:23
  9.6 31.1 %collective-permute-start = (bf16[128,6144]{1,0:T(8,128)(2,1)}, bf16[128,6144]{1,0:T(8,128)(2,1)S(1)}, u32[]{:S(2)}, u32[]{:S(2)}) collective-permute-start(bf16[128,6144]{1,0:T(8,128)(2,1)} %get-tuple-element.21), channel_id=1, source_target_pairs={{0,1},{1,2},{2,3},{3,4},{4,5},{5,6},{6,7},{7,8},{8,9},{9,10},{10,1... | collective-permute-start | bytes 4718600 | tf_op jit(solution)/shard_map/ppermute | solution.py:23
  14.1 26.6 %collective-permute-start.3 = (bf16[128,6144]{1,0:T(8,128)(2,1)}, bf16[128,6144]{1,0:T(8,128)(2,1)}, u32[]{:S(2)}, u32[]{:S(2)}) collective-permute-start(bf16[128,6144]{1,0:T(8,128)(2,1)} %collective-permute-done.2), channel_id=1, source_target_pairs={{6,4},{10,8},{14,12},{22,20},{26,24},{30,28}} | collective-permute-start | bytes 4718600 | tf_op jit(solution)/shard_map/ppermute | solution.py:23
  84.3 42.9 %all-to-all-start.4 = ((bf16[8,4,128,256]{3,2,1,0:T(8,128)(2,1)}), bf16[8,4,128,256]{3,2,1,0:T(8,128)(2,1)S(1)}, u32[]{:S(2)}, u32[]{:S(2)}) async-start(bf16[8,4,128,256]{3,2,1,0:T(8,128)(2,1)} %transform.9), calls=%async_computation.4 | async-start | bytes 4194304 | tf_op jit(solution)/shard_map/all_to_all | solution.py:289
  128.6 29.2 %all-to-all-start = ((bf16[8,4,128,256]{3,2,1,0:T(8,128)(2,1)}), bf16[8,4,128,256]{3,2,1,0:T(8,128)(2,1)S(1)}, u32[]{:S(2)}, u32[]{:S(2)}) async-start(bf16[8,4,128,256]{3,2,1,0:T(8,128)(2,1)} %transform.5), calls=%async_computation | async-start | bytes 4194304 | tf_op jit(solution)/shard_map/all_to_all | solution.py:289
  159.2 42.3 %all-to-all-start.1 = ((bf16[8,4,192,256]{3,2,1,0:T(8,128)(2,1)}), bf16[8,4,192,256]{3,2,1,0:T(8,128)(2,1)S(1)}, u32[]{:S(2)}, u32[]{:S(2)}) async-start(bf16[8,4,192,256]{3,2,1,0:T(8,128)(2,1)} %transform.6), calls=%async_computation.1 | async-start | bytes 6291456 | tf_op jit(solution)/shard_map/all_to_all | solution.py:289
  162.9 43.3 %collective-permute-start.10 = (bf16[8,128,256]{2,1,0:T(8,128)(2,1)}, bf16[8,128,256]{2,1,0:T(8,128)(2,1)}, u32[]{:S(2)}, u32[]{:S(2)}) collective-permute-start(bf16[8,128,256]{2,1,0:T(8,128)(2,1)} %get-tuple-element.26), channel_id=1, source_target_pairs={{0,4},{1,5},{2,6},{3,7},{4,0},{5,1},{6,2},{7,3},{8,12},{9,13},{10,... | collective-permute-start | bytes 1572872 | tf_op jit(solution)/shard_map/ppermute | solution.py:282
  171.9 43.4 %collective-permute-start.11 = (bf16[8,128,256]{2,1,0:T(8,128)(2,1)}, bf16[8,128,256]{2,1,0:T(8,128)(2,1)}, u32[]{:S(2)}, u32[]{:S(2)}) collective-permute-start(bf16[8,128,256]{2,1,0:T(8,128)(2,1)} %get-tuple-element.27), channel_id=1, source_target_pairs={{0,8},{1,9},{2,10},{3,11},{4,12},{5,13},{6,14},{7,15},{8,0},{9,1},... | collective-permute-start | bytes 1572872 | tf_op jit(solution)/shard_map/ppermute | solution.py:282
  174.5 45.3 %collective-permute-start.12 = (bf16[8,128,256]{2,1,0:T(8,128)(2,1)}, bf16[8,128,256]{2,1,0:T(8,128)(2,1)}, u32[]{:S(2)}, u32[]{:S(2)}) collective-permute-start(bf16[8,128,256]{2,1,0:T(8,128)(2,1)} %get-tuple-element.28), channel_id=1, source_target_pairs={{0,12},{1,13},{2,14},{3,15},{4,8},{5,9},{6,10},{7,11},{8,4},{9,5},... | collective-permute-start | bytes 1572872 | tf_op jit(solution)/shard_map/ppermute | solution.py:282
  201.5 100.7 %all-to-all-start.3 = ((bf16[8,4,192,256]{3,2,1,0:T(8,128)(2,1)}), bf16[8,4,192,256]{3,2,1,0:T(8,128)(2,1)}, u32[]{:S(2)}, u32[]{:S(2)}) async-start(bf16[8,4,192,256]{3,2,1,0:T(8,128)(2,1)} %transform.8), calls=%async_computation.3 | async-start | bytes 6291456 | tf_op jit(solution)/shard_map/all_to_all | solution.py:289
  208.1 38.2 %collective-permute-start.13 = (bf16[8,128,256]{2,1,0:T(8,128)(2,1)}, bf16[8,128,256]{2,1,0:T(8,128)(2,1)}, u32[]{:S(2)}, u32[]{:S(2)}) collective-permute-start(bf16[8,128,256]{2,1,0:T(8,128)(2,1)} %get-tuple-element.30), channel_id=1, source_target_pairs={{0,4},{1,5},{2,6},{3,7},{4,0},{5,1},{6,2},{7,3},{8,12},{9,13},{10,... | collective-permute-start | bytes 1572872 | tf_op jit(solution)/shard_map/ppermute | solution.py:282
  217.2 32.1 %collective-permute-start.14 = (bf16[8,128,256]{2,1,0:T(8,128)(2,1)}, bf16[8,128,256]{2,1,0:T(8,128)(2,1)}, u32[]{:S(2)}, u32[]{:S(2)}) collective-permute-start(bf16[8,128,256]{2,1,0:T(8,128)(2,1)} %get-tuple-element.31), channel_id=1, source_target_pairs={{0,8},{1,9},{2,10},{3,11},{4,12},{5,13},{6,14},{7,15},{8,0},{9,1},... | collective-permute-start | bytes 1572872 | tf_op jit(solution)/shard_map/ppermute | solution.py:282
  240.1 16.8 %collective-permute-start.15 = (bf16[8,128,256]{2,1,0:T(8,128)(2,1)}, bf16[8,128,256]{2,1,0:T(8,128)(2,1)S(1)}, u32[]{:S(2)}, u32[]{:S(2)}) collective-permute-start(bf16[8,128,256]{2,1,0:T(8,128)(2,1)} %get-tuple-element.32), channel_id=1, source_target_pairs={{0,12},{1,13},{2,14},{3,15},{4,8},{5,9},{6,10},{7,11},{8,4},{9,5},... | collective-permute-start | bytes 1572872 | tf_op jit(solution)/shard_map/ppermute | solution.py:282
  240.1 26.4 %collective-permute-start.16 = (bf16[8,128,256]{2,1,0:T(8,128)(2,1)}, bf16[8,128,256]{2,1,0:T(8,128)(2,1)S(1)}, u32[]{:S(2)}, u32[]{:S(2)}) collective-permute-start(bf16[8,128,256]{2,1,0:T(8,128)(2,1)} %get-tuple-element.34), channel_id=1, source_target_pairs={{0,4},{1,5},{2,6},{3,7},{4,0},{5,1},{6,2},{7,3},{8,12},{9,13},{10,... | collective-permute-start | bytes 1572872 | tf_op jit(solution)/shard_map/ppermute | solution.py:282
  243.2 57.4 %collective-permute-start.17 = (bf16[8,128,256]{2,1,0:T(8,128)(2,1)}, bf16[8,128,256]{2,1,0:T(8,128)(2,1)S(1)}, u32[]{:S(2)}, u32[]{:S(2)}) collective-permute-start(bf16[8,128,256]{2,1,0:T(8,128)(2,1)} %get-tuple-element.35), channel_id=1, source_target_pairs={{0,8},{1,9},{2,10},{3,11},{4,12},{5,13},{6,14},{7,15},{8,0},{9,1},... | collective-permute-start | bytes 1572872 | tf_op jit(solution)/shard_map/ppermute | solution.py:282
  246.3 55.1 %collective-permute-start.18 = (bf16[8,128,256]{2,1,0:T(8,128)(2,1)}, bf16[8,128,256]{2,1,0:T(8,128)(2,1)S(1)}, u32[]{:S(2)}, u32[]{:S(2)}) collective-permute-start(bf16[8,128,256]{2,1,0:T(8,128)(2,1)} %get-tuple-element.36), channel_id=1, source_target_pairs={{0,12},{1,13},{2,14},{3,15},{4,8},{5,9},{6,10},{7,11},{8,4},{9,5},... | collective-permute-start | bytes 1572872 | tf_op jit(solution)/shard_map/ppermute | solution.py:282
  302.3 214.3 %all-to-all-start.2 = ((bf16[8,12,128,256]{3,2,1,0:T(8,128)(2,1)}), bf16[8,12,128,256]{3,2,1,0:T(8,128)(2,1)}, u32[]{:S(2)}, u32[]{:S(2)}) async-start(bf16[8,12,128,256]{3,2,1,0:T(8,128)(2,1)} %bitcast_dynamic-update-slice_fusion), calls=%async_computation.2 | async-start | bytes 12582912 | tf_op jit(solution)/shard_map/all_to_all | solution.py:289
  309.5 19.4 %collective-permute-start.24 = (bf16[8,128,256]{2,1,0:T(8,128)(2,1)S(1)}, bf16[8,128,256]{2,1,0:T(8,128)(2,1)S(1)}, u32[]{:S(2)}, u32[]{:S(2)}) collective-permute-start(bf16[8,128,256]{2,1,0:T(8,128)(2,1)S(1)} %get-tuple-element.45), channel_id=1, source_target_pairs={{0,12},{1,13},{2,14},{3,15},{4,8},{5,9},{6,10},{7,11},{8,4},{9,5},... | collective-permute-start | bytes 1572872 | tf_op jit(solution)/shard_map/ppermute | solution.py:282
  312.0 81.0 %collective-permute-start.23 = (bf16[8,128,256]{2,1,0:T(8,128)(2,1)S(1)}, bf16[8,128,256]{2,1,0:T(8,128)(2,1)S(1)}, u32[]{:S(2)}, u32[]{:S(2)}) collective-permute-start(bf16[8,128,256]{2,1,0:T(8,128)(2,1)S(1)} %get-tuple-element.46), channel_id=1, source_target_pairs={{0,8},{1,9},{2,10},{3,11},{4,12},{5,13},{6,14},{7,15},{8,0},{9,1},... | collective-permute-start | bytes 1572872 | tf_op jit(solution)/shard_map/ppermute | solution.py:282
  320.9 123.2 %copy-start.3 = (bf16[8,4,128,256]{3,2,1,0:T(8,128)(2,1)S(1)}, bf16[8,4,128,256]{3,2,1,0:T(8,128)(2,1)}, u32[]{:S(2)}) copy-start(bf16[8,4,128,256]{3,2,1,0:T(8,128)(2,1)} %copy-done.2) | copy-start | bytes 6291460
  320.9 74.6 %collective-permute-start.22 = (bf16[8,128,256]{2,1,0:T(8,128)(2,1)S(1)}, bf16[8,128,256]{2,1,0:T(8,128)(2,1)S(1)}, u32[]{:S(2)}, u32[]{:S(2)}) collective-permute-start(bf16[8,128,256]{2,1,0:T(8,128)(2,1)S(1)} %get-tuple-element.47), channel_id=1, source_target_pairs={{0,4},{1,5},{2,6},{3,7},{4,0},{5,1},{6,2},{7,3},{8,12},{9,13},{10,... | collective-permute-start | bytes 1572872 | tf_op jit(solution)/shard_map/ppermute | solution.py:282
  324.2 71.4 %collective-permute-start.21 = (bf16[8,192,256]{2,1,0:T(8,128)(2,1)S(1)}, bf16[8,192,256]{2,1,0:T(8,128)(2,1)S(1)}, u32[]{:S(2)}, u32[]{:S(2)}) collective-permute-start(bf16[8,192,256]{2,1,0:T(8,128)(2,1)S(1)} %get-tuple-element.37), channel_id=1, source_target_pairs={{0,12},{1,13},{2,14},{3,15},{4,8},{5,9},{6,10},{7,11},{8,4},{9,5},... | collective-permute-start | bytes 2359304 | tf_op jit(solution)/shard_map/ppermute | solution.py:282
  326.6 133.9 %collective-permute-start.20 = (bf16[8,192,256]{2,1,0:T(8,128)(2,1)S(1)}, bf16[8,192,256]{2,1,0:T(8,128)(2,1)S(1)}, u32[]{:S(2)}, u32[]{:S(2)}) collective-permute-start(bf16[8,192,256]{2,1,0:T(8,128)(2,1)S(1)} %get-tuple-element.38), channel_id=1, source_target_pairs={{0,8},{1,9},{2,10},{3,11},{4,12},{5,13},{6,14},{7,15},{8,0},{9,1},... | collective-permute-start | bytes 2359304 | tf_op jit(solution)/shard_map/ppermute | solution.py:282
  328.9 134.1 %copy-start.11 = (bf16[8,128,256]{2,1,0:T(8,128)(2,1)}, bf16[8,128,256]{2,1,0:T(8,128)(2,1)S(1)}, u32[]{:S(2)}) copy-start(bf16[8,128,256]{2,1,0:T(8,128)(2,1)S(1)} %collective-permute-done.24) | copy-start | bytes 1572868
  328.9 134.1 %collective-permute-start.19 = (bf16[8,192,256]{2,1,0:T(8,128)(2,1)S(1)}, bf16[8,192,256]{2,1,0:T(8,128)(2,1)S(1)}, u32[]{:S(2)}, u32[]{:S(2)}) collective-permute-start(bf16[8,192,256]{2,1,0:T(8,128)(2,1)S(1)} %get-tuple-element.39), channel_id=1, source_target_pairs={{0,4},{1,5},{2,6},{3,7},{4,0},{5,1},{6,2},{7,3},{8,12},{9,13},{10,... | collective-permute-start | bytes 2359304 | tf_op jit(solution)/shard_map/ppermute | solution.py:282
  393.0 70.0 %collective-permute-start.9 = (bf16[8,192,256]{2,1,0:T(8,128)(2,1)S(1)}, bf16[8,192,256]{2,1,0:T(8,128)(2,1)S(1)}, u32[]{:S(2)}, u32[]{:S(2)}) collective-permute-start(bf16[8,192,256]{2,1,0:T(8,128)(2,1)S(1)} %get-tuple-element.41), channel_id=1, source_target_pairs={{0,12},{1,13},{2,14},{3,15},{4,8},{5,9},{6,10},{7,11},{8,4},{9,5},... | collective-permute-start | bytes 2359304 | tf_op jit(solution)/shard_map/ppermute | solution.py:282
  395.5 138.8 %collective-permute-start.8 = (bf16[8,192,256]{2,1,0:T(8,128)(2,1)}, bf16[8,192,256]{2,1,0:T(8,128)(2,1)S(1)}, u32[]{:S(2)}, u32[]{:S(2)}) collective-permute-start(bf16[8,192,256]{2,1,0:T(8,128)(2,1)} %get-tuple-element.42), channel_id=1, source_target_pairs={{0,8},{1,9},{2,10},{3,11},{4,12},{5,13},{6,14},{7,15},{8,0},{9,1},... | collective-permute-start | bytes 2359304 | tf_op jit(solution)/shard_map/ppermute | solution.py:282
  395.6 138.8 %collective-permute-start.7 = (bf16[8,192,256]{2,1,0:T(8,128)(2,1)}, bf16[8,192,256]{2,1,0:T(8,128)(2,1)S(1)}, u32[]{:S(2)}, u32[]{:S(2)}) collective-permute-start(bf16[8,192,256]{2,1,0:T(8,128)(2,1)} %get-tuple-element.43), channel_id=1, source_target_pairs={{0,4},{1,5},{2,6},{3,7},{4,0},{5,1},{6,2},{7,3},{8,12},{9,13},{10,... | collective-permute-start | bytes 2359304 | tf_op jit(solution)/shard_map/ppermute | solution.py:282
  460.5 84.3 %collective-permute-start.6 = (bf16[8,128,256]{2,1,0:T(8,128)(2,1)}, bf16[8,128,256]{2,1,0:T(8,128)(2,1)}, u32[]{:S(2)}, u32[]{:S(2)}) collective-permute-start(bf16[8,128,256]{2,1,0:T(8,128)(2,1)} %get-tuple-element.49), channel_id=1, source_target_pairs={{0,12},{1,13},{2,14},{3,15},{4,8},{5,9},{6,10},{7,11},{8,4},{9,5},... | collective-permute-start | bytes 1572872 | tf_op jit(solution)/shard_map/ppermute | solution.py:282
  463.0 81.8 %collective-permute-start.5 = (bf16[8,128,256]{2,1,0:T(8,128)(2,1)}, bf16[8,128,256]{2,1,0:T(8,128)(2,1)}, u32[]{:S(2)}, u32[]{:S(2)}) collective-permute-start(bf16[8,128,256]{2,1,0:T(8,128)(2,1)} %get-tuple-element.50), channel_id=1, source_target_pairs={{0,8},{1,9},{2,10},{3,11},{4,12},{5,13},{6,14},{7,15},{8,0},{9,1},... | collective-permute-start | bytes 1572872 | tf_op jit(solution)/shard_map/ppermute | solution.py:282
  463.0 81.8 %collective-permute-start.4 = (bf16[8,128,256]{2,1,0:T(8,128)(2,1)}, bf16[8,128,256]{2,1,0:T(8,128)(2,1)}, u32[]{:S(2)}, u32[]{:S(2)}) collective-permute-start(bf16[8,128,256]{2,1,0:T(8,128)(2,1)} %get-tuple-element.51), channel_id=1, source_target_pairs={{0,4},{1,5},{2,6},{3,7},{4,0},{5,1},{6,2},{7,3},{8,12},{9,13},{10,... | collective-permute-start | bytes 1572872 | tf_op jit(solution)/shard_map/ppermute | solution.py:282
  (12 other events, 361.0 us)
where the time goes:
time: 553 us; the launch traced here: 552 us
  Pallas kernels  208 us (38%)
  starting transfers between devices  197 us (36%)
  waiting for transfers between devices  113 us (20%)
  local copies, waits for them, and re-layouts  32.8 us (6%)
    ppermute x21, starting transfers between devices, across(): return lax.ppermute(value, 'tm', pairs)  153 us
    pallas_call x5, Pallas kernels, on_device(): value = call(plane, early, late, coarse, fine)  105 us
    ppermute x21, waiting for transfers between devices, across(): return lax.ppermute(value, 'tm', pairs)  104 us
    pallas_call x6, Pallas kernels, on_device(): pl.pallas_call(lambda *refs, block_inp=block_inp, sources=sources: correl...  50 us
    pallas_call x2, Pallas kernels, filtered_half(): pl.pallas_call(lambda *refs: filter_kernel(*refs, history=len(history), c...  47.8 us
    all_to_all x5, starting transfers between devices, within(): lax.all_to_all(value, ('inp', 'tm'), split_axis=0, concat_axis=0, axis_in...  33.9 us
    unnamed x39, local copies, waits for them, and re-layouts  23.4 us
  transfers between devices with their start and end apart: 30, of which 7 were waited for; matrix products, arithmetic and copies ran while one was open for 5% of the time, Pallas kernels for 28%

commit v1 on v0

--- a/solution.py
+++ b/solution.py
@@ -10,7 +10,7 @@
 
 
 INNER = 4
-CHANNEL_STEPS = (8, 4, 4, 6, 6, 4)
+CHANNEL_STEPS = (8, 4, 4, 4, 7, 5)
 HEAD_TERMS = 1
 CHUNK = 512
 Z_FIRST_GROUPS = 1
@@ -31,7 +31,9 @@
         around = send(high, [(d - 1, d + via) for d in edges])
         around = send(around, [(d + via, d) for d in edges])
     high = send(high, [(d, d + 1) for d in range(count - 1) if not detour or (d + 1) % inner])
-    return low, high, around if detour else high
+    if detour:
+        high = jnp.where(lax.axis_index("tm") % inner == 0, around, high)
+    return low, high
 
 
 def turn_tables(angles, frame_len):
@@ -102,9 +104,11 @@
     high[...] = samples[half:].astype(F32).astype(BF16)
 
 
-def filter_kernel(plane, *refs, history, count, keep):
-    old, refs = refs[:history], refs[history:]
-    samples, taps, coarse, fine, filtered, *outs, table, spread, recent, current = refs
+def filter_kernel(plane, *refs, count, keep):
+    old, (samples, taps, coarse, fine), refs = refs[:keep], refs[keep : keep + 4], refs[keep + 4 :]
+    if len(refs) > 5 + coarse.shape[0]:
+        refs = refs[1:]
+    filtered, *outs, table, spread, recent, current = refs
     step = pl.program_id(0)
     inputs, frame_len = samples.shape
     width = min(256, frame_len)
@@ -114,19 +118,7 @@
     def _():
         build_table(plane, coarse, fine, table, 0, count)
         for k in range(keep):
-            if history == keep:
-                recent[k] = old[k][...].astype(F32).astype(BF16)
-                continue
-            low, high, around = old[3 * k : 3 * k + 3]
-            recent[k, : inputs // 2] = low[...]
-
-            @pl.when(plane[1] == 0)
-            def _():
-                recent[k, inputs // 2 :] = around[...]
-
-            @pl.when(plane[1] != 0)
-            def _():
-                recent[k, inputs // 2 :] = high[...]
+            recent[k] = old[k][...].astype(F32).astype(BF16)
 
     slots = [lax.rem(step + k, keep) for k in range(keep)]
 
@@ -216,7 +208,7 @@
     points = np.arange(frame_len)
     coarse = jnp.asarray(turn_tables(owner_ids[..., None] * chan_dev * points % frame_len, frame_len))
     fine = jnp.asarray(turn_tables(np.arange(chan_dev)[:, None] * points % frame_len, frame_len))
-    plane = jnp.stack([lax.axis_index("tm") // inner, lax.axis_index("tm") % inner]).astype(jnp.int32)
+    plane = (lax.axis_index("tm") // inner).astype(jnp.int32).reshape(1)
 
     head = min(CHANNEL_STEPS[0], chan_dev)
     bounds = [0]
@@ -252,30 +244,46 @@
     tables = [whole(*coarse.shape), whole(*fine.shape)]
     frame_spec = pl.BlockSpec((1, local_inputs, frame_len), lambda s: (s, 0, 0))
 
-    def at_frame(index, count=local_inputs):
-        return pl.BlockSpec((count, frame_len), lambda s: (0, index), pipeline_mode=once)
-
-    def filtered_half(first, history, history_specs):
-        piece = jax.ShapeDtypeStruct((places, 16 * head, local_inputs), BF16)
+    parts = 2 if local_inputs % 256 == 0 else 1
+    part_inputs = local_inputs // parts
+
+    def filtered_half(first, history, history_block, part, filled):
+        piece = jax.ShapeDtypeStruct((places, 16 * head, part_inputs), BF16)
+        operands = [plane, *[history] * keep, samples, filter_taps, coarse, fine]
+        specs = [
+            scalar,
+            *[
+                pl.BlockSpec(
+                    (part_inputs, frame_len),
+                    lambda s, k=k: (history_block[0], history_block[1] + k),
+                    pipeline_mode=once,
+                )
+                for k in range(keep)
+            ],
+            pl.BlockSpec((part_inputs, frame_len), lambda s: (part, first + s)),
+            whole(tap_count, frame_len),
+            *tables,
+        ]
+        if filled is not None:
+            operands.append(filled)
+            specs.append(pl.BlockSpec(memory_space=pl.ANY))
+        rows = 2 * head * owners
         return pl.pallas_call(
-            lambda *refs: filter_kernel(*refs, history=len(history), count=head, keep=keep),
+            lambda *refs: filter_kernel(*refs, count=head, keep=keep),
             grid=(half,),
-            in_specs=[
-                scalar,
-                *history_specs,
-                pl.BlockSpec((local_inputs, frame_len), lambda s: (0, first + s)),
-                whole(tap_count, frame_len),
-                *tables,
-            ],
-            out_specs=[frame_spec] + [whole(*piece.shape)] * z_count,
+            in_specs=specs,
+            out_specs=[pl.BlockSpec((1, part_inputs, frame_len), lambda s: (s, part, 0))]
+            + [whole(*piece.shape)] * z_count,
             out_shape=[jax.ShapeDtypeStruct((half, local_inputs, frame_len), BF16)] + [piece] * z_count,
             scratch_shapes=[
-                *scratch(head, 1, HEAD_TERMS),
-                pltpu.VMEM((keep, local_inputs, frame_len), BF16),
-                pltpu.VMEM((local_inputs, frame_len), BF16),
+                pltpu.VMEM((HEAD_TERMS * rows, frame_len), BF16),
+                pltpu.VMEM((part_inputs // min(128, part_inputs), rows * 8, min(128, part_inputs)), F32),
+                pltpu.VMEM((keep, part_inputs, frame_len), BF16),
+                pltpu.VMEM((part_inputs, frame_len), BF16),
             ],
+            input_output_aliases={} if filled is None else {len(operands) - 1: 0},
             name="filter_transform",
-        )(plane, *history, samples, filter_taps, coarse, fine)
+        )(*operands)
 
     def across(value, k):
         pairs = [(z * inner + i, (z ^ k) * inner + i) for z in range(z_count) for i in range(inner)]
@@ -285,19 +293,32 @@
         [x * tm_count + z * inner + i for x in range(inp_count) for i in range(inner)] for z in range(z_count)
     ]
 
+    exchanged = []
+
     def within(value):
-        return lax.all_to_all(
+        if exchanged:
+            value, _ = lax.optimization_barrier((value, exchanged[-1]))
+        moved = lax.all_to_all(
             value, ("inp", "tm"), split_axis=0, concat_axis=0, axis_index_groups=plane_groups, tiled=True
         )
+        exchanged.append(moved)
+        return moved
 
     def z_stage(pieces):
         return [pieces[0]] + [across(pieces[k], k) for k in range(1, z_count)]
 
-    late, *late_pieces = filtered_half(half, [samples] * keep, [at_frame(half - keep + k) for k in range(keep)])
-    z_first = z_stage(late_pieces)
-    halo_specs = [at_frame(k, local_inputs // 2) for k in range(keep) for _ in range(3)]
-    early, *early_pieces = filtered_half(0, list(halo) * keep, halo_specs)
-    z_first += z_stage(early_pieces)
+    def head_half(first, histories, blocks):
+        filtered, moved = None, []
+        for part in range(parts):
+            filtered, *pieces = filtered_half(first, histories[part], blocks[part], part, filtered)
+            moved.append(z_stage(pieces))
+        return filtered, [jnp.concatenate(each, axis=2) if parts > 1 else each[0] for each in zip(*moved)]
+
+    late, z_first = head_half(half, [samples] * parts, [(part, half - keep) for part in range(parts)])
+    if parts == 1:
+        halo = [jnp.concatenate(halo, axis=0)]
+    early, more = head_half(0, halo, [(0, 0)] * parts)
+    z_first += more
 
     arrived = {}
     z_first_groups = [(0, head, 1, 2 * z_count, 0)]

time: 553 us -> 619 us (1.12)
  waiting for transfers between devices: 113 us -> 178 us
  local copies, waits for them, and re-layouts: 32.8 us -> 16.7 us
  other arithmetic: 0.64 us -> 13.8 us
  Pallas kernels: 208 us -> 219 us
  starting transfers between devices: 197 us -> 189 us
    ppermute x21 -> x27, waiting for transfers between devices: 104 us -> 148 us  [across(): return lax.ppermute(value, 'tm', pairs)]
    all_to_all x5, waiting for transfers between devices: 8.07 us -> 30.1 us  [within(): lax.all_to_all(value, ('inp', 'tm'), split_axis=0, concat_axis=0, axis_in...]
    unnamed x39 -> x31, local copies, waits for them, and re-layouts: 23.4 us -> 7.09 us
    pallas_call x2 -> x4, Pallas kernels: 47.8 us -> 63.1 us  [filtered_half(): pl.pallas_call(lambda *refs: filter_kernel(*refs, count=head, keep=keep),...]
    unnamed x0 -> x8, other arithmetic: none -> 11.1 us
    ppermute x21 -> x27, starting transfers between devices: 153 us -> 146 us  [across(): return lax.ppermute(value, 'tm', pairs)]
  transfers between devices with their start and end apart: 30 -> 36, of which waited for: 7 -> 13; matrix products, arithmetic and copies ran while one was open for 5% -> 4% of each run, Pallas kernels for 28% -> 28%
where the time goes in v1:
time: 619 us; the launch traced here: 617 us
  Pallas kernels  219 us (35%)
  starting transfers between devices  189 us (31%)
  waiting for transfers between devices  178 us (29%)
  local copies, waits for them, and re-layouts  16.7 us (3%)
  other arithmetic  13.8 us (2%)
    ppermute x27, waiting for transfers between devices, across(): return lax.ppermute(value, 'tm', pairs)  148 us
    ppermute x27, starting transfers between devices, across(): return lax.ppermute(value, 'tm', pairs)  146 us
    pallas_call x5, Pallas kernels, on_device(): value = call(plane, early, late, coarse, fine)  101 us
    pallas_call x4, Pallas kernels, filtered_half(): pl.pallas_call(lambda *refs: filter_kernel(*refs, count=head, keep=keep),...  63.1 us
    pallas_call x6, Pallas kernels, on_device(): pl.pallas_call(lambda *refs, block_inp=block_inp, sources=sources: correl...  49.6 us
    all_to_all x5, starting transfers between devices, within(): lax.all_to_all(value, ('inp', 'tm'), split_axis=0, concat_axis=0, axis_in...  32.5 us
    all_to_all x5, waiting for transfers between devices, within(): lax.all_to_all(value, ('inp', 'tm'), split_axis=0, concat_axis=0, axis_in...  30.1 us
  transfers between devices with their start and end apart: 36, of which 13 were waited for; matrix products, arithmetic and copies ran while one was open for 4% of the time, Pallas kernels for 28%

profile of v1, /device:TPU:0, one launch (start us, length us, event | category | flops | bytes accessed | tf_op | source)
XLA Modules:
  0.0 616.6 jit_solution(17666297089353640469)
XLA Ops:
  16.0 16.1 %filter_transform.6 = (bf16[8,256,2048]{2,1,0:T(8,128)(2,1)}, bf16[8,128,128]{2,1,0:T(8,128)(2,1)}, bf16[8,128,128]{2,1,0:T(8,128)(2,1)}, bf16[8,128,128]{2,1,0:T(8,128)(2,1)}, bf16[8,128,128]{2,1,0:T(8,128)(2,1)}) custom-call(s32[1]{0:T(128)} %bitcast.refs_0_, s32[256,32768]{1,0:T(8,128)} %refs_4_.12, s32[256,32768]{1,0:T(8,128)} %refs_4_.12, ...), custom_call_target="tpu_custom_call" | custom-call | tf_op jit(solution)/shard_map/filter_transform/pallas_call | solution.py:271
  32.1 16.1 %filter_transform.7 = (bf16[8,256,2048]{2,1,0:T(8,128)(2,1)}, bf16[8,128,128]{2,1,0:T(8,128)(2,1)}, bf16[8,128,128]{2,1,0:T(8,128)(2,1)}, bf16[8,128,128]{2,1,0:T(8,128)(2,1)}, bf16[8,128,128]{2,1,0:T(8,128)(2,1)}) custom-call(s32[1]{0:T(128)} %bitcast.refs_0_, s32[256,32768]{1,0:T(8,128)} %refs_4_.12, ...), custom_call_target="tpu_custom_call", output_to_operand_aliasing={{0}: (8, {})} | custom-call | tf_op jit(solution)/shard_map/filter_transform/pallas_call | solution.py:271
  49.4 15.4 %filter_transform.4 = (bf16[8,256,2048]{2,1,0:T(8,128)(2,1)}, bf16[8,128,128]{2,1,0:T(8,128)(2,1)}, bf16[8,128,128]{2,1,0:T(8,128)(2,1)}, bf16[8,128,128]{2,1,0:T(8,128)(2,1)}, bf16[8,128,128]{2,1,0:T(8,128)(2,1)}) custom-call(s32[1]{0:T(128)} %bitcast.refs_0_, bf16[128,6144]{1,0:T(8,128)(2,1)} %copy-done, bf16[128,6144]{1,0:T(8,128)(2,1)} %copy-done, ...), custom_call_target="tpu_custom_call" | custom-call | tf_op jit(solution)/shard_map/filter_transform/pallas_call | solution.py:271
  67.5 15.4 %filter_transform.5 = (bf16[8,256,2048]{2,1,0:T(8,128)(2,1)}, bf16[8,128,128]{2,1,0:T(8,128)(2,1)}, bf16[8,128,128]{2,1,0:T(8,128)(2,1)}, bf16[8,128,128]{2,1,0:T(8,128)(2,1)}, bf16[8,128,128]{2,1,0:T(8,128)(2,1)}) custom-call(s32[1]{0:T(128)} %bitcast.refs_0_, ...), custom_call_target="tpu_custom_call", output_to_operand_aliasing={{0}: (8, {})} | custom-call | tf_op jit(solution)/shard_map/filter_transform/pallas_call | solution.py:271
  83.0 18.1 %transform.8 = bf16[8,4,128,256]{3,2,1,0:T(8,128)(2,1)} custom-call(s32[1]{0:T(128)} %bitcast.refs_0_, bf16[8,256,2048]{2,1,0:T(8,128)(2,1)} %get-tuple-element.38.refs_1_, bf16[8,256,2048]{2,1,0:T(8,128)(2,1)} %get-tuple-element.40.refs_2_, f32[4,2,8,2048]{3,2,1,0:T(8,128)} %constant.35.clone.refs_6_.refs_3_, f32[2,32,2048]{2,1,0:T(8,128)} %constant.36.clone.refs_7_.refs_4_), custom_call_target="tpu_custom_call" | custom-call | tf_op jit(solution)/shard_map/transform/pallas_call | solution.py:341
  101.1 15.8 %all-to-all-start = ((bf16[8,4,128,256]{3,2,1,0:T(8,128)(2,1)}), bf16[8,4,128,256]{3,2,1,0:T(8,128)(2,1)S(1)}, u32[]{:S(2)}, u32[]{:S(2)}) async-start(bf16[8,4,128,256]{3,2,1,0:T(8,128)(2,1)} %transform.8), calls=%async_computation | async-start | bytes 4194304 | tf_op jit(solution)/shard_map/all_to_all | solution.py:301
  116.9 18.1 %transform.7 = bf16[8,4,128,256]{3,2,1,0:T(8,128)(2,1)} custom-call(s32[1]{0:T(128)} %bitcast.refs_0_, bf16[8,256,2048]{2,1,0:T(8,128)(2,1)} %get-tuple-element.38.refs_1_, bf16[8,256,2048]{2,1,0:T(8,128)(2,1)} %get-tuple-element.40.refs_2_, f32[4,2,8,2048]{3,2,1,0:T(8,128)} %constant.35.clone.refs_6_.refs_3_, f32[2,32,2048]{2,1,0:T(8,128)} %constant.36.clone.refs_7_.refs_4_), custom_call_target="tpu_custom_call" | custom-call | tf_op jit(solution)/shard_map/transform/pallas_call | solution.py:341
  134.9 7.6 %all-to-all-done = bf16[8,4,128,256]{3,2,1,0:T(8,128)(2,1)S(1)} async-done(((bf16[8,4,128,256]{3,2,1,0:T(8,128)(2,1)}), bf16[8,4,128,256]{3,2,1,0:T(8,128)(2,1)S(1)}, u32[]{:S(2)}, u32[]{:S(2)}) %all-to-all-start) | async-done | bytes 2097184 | tf_op jit(solution)/shard_map/all_to_all | solution.py:301
  147.6 26.3 %transform.6 = bf16[8,4,224,256]{3,2,1,0:T(8,128)(2,1)} custom-call(s32[1]{0:T(128)} %bitcast.refs_0_, bf16[8,256,2048]{2,1,0:T(8,128)(2,1)} %get-tuple-element.38.refs_1_, bf16[8,256,2048]{2,1,0:T(8,128)(2,1)} %get-tuple-element.40.refs_2_, f32[4,2,8,2048]{3,2,1,0:T(8,128)} %constant.35.clone.refs_6_.refs_3_, f32[2,32,2048]{2,1,0:T(8,128)} %constant.36.clone.refs_7_.refs_4_), custom_call_target="tpu_custom_call" | custom-call | tf_op jit(solution)/shard_map/transform/pallas_call | solution.py:341
  178.4 20.1 %transform.5 = bf16[8,4,160,256]{3,2,1,0:T(8,128)(2,1)} custom-call(s32[1]{0:T(128)} %bitcast.refs_0_, bf16[8,256,2048]{2,1,0:T(8,128)(2,1)} %get-tuple-element.38.refs_1_, bf16[8,256,2048]{2,1,0:T(8,128)(2,1)} %get-tuple-element.40.refs_2_, f32[4,2,8,2048]{3,2,1,0:T(8,128)} %constant.35.clone.refs_6_.refs_3_, f32[2,32,2048]{2,1,0:T(8,128)} %constant.36.clone.refs_7_.refs_4_), custom_call_target="tpu_custom_call" | custom-call | tf_op jit(solution)/shard_map/transform/pallas_call | solution.py:341
  198.5 22.4 %all-to-all-done.2 = bf16[8,4,224,256]{3,2,1,0:T(8,128)(2,1)} async-done(((bf16[8,4,224,256]{3,2,1,0:T(8,128)(2,1)}), bf16[8,4,224,256]{3,2,1,0:T(8,128)(2,1)}, u32[]{:S(2)}, u32[]{:S(2)}) %all-to-all-start.2) | async-done | bytes 3670048 | tf_op jit(solution)/shard_map/all_to_all | solution.py:301
  235.2 11.1 %collective-permute-done.10 = bf16[8,128,128]{2,1,0:T(8,128)(2,1)S(1)} collective-permute-done((bf16[8,128,128]{2,1,0:T(8,128)(2,1)}, bf16[8,128,128]{2,1,0:T(8,128)(2,1)S(1)}, u32[]{:S(2)}, u32[]{:S(2)}) %collective-permute-start.10) | collective-permute-done | bytes 262176 | tf_op jit(solution)/shard_map/ppermute | solution.py:290
  254.5 12.4 %collective-permute-done.13 = bf16[8,128,128]{2,1,0:T(8,128)(2,1)S(1)} collective-permute-done((bf16[8,128,128]{2,1,0:T(8,128)(2,1)}, bf16[8,128,128]{2,1,0:T(8,128)(2,1)S(1)}, u32[]{:S(2)}, u32[]{:S(2)}) %collective-permute-start.13) | collective-permute-done | bytes 262176 | tf_op jit(solution)/shard_map/ppermute | solution.py:290
  267.7 7.7 %collective-permute-start.19 = (bf16[8,128,128]{2,1,0:T(8,128)(2,1)}, bf16[8,128,128]{2,1,0:T(8,128)(2,1)}, u32[]{:S(2)}, u32[]{:S(2)}) collective-permute-start(bf16[8,128,128]{2,1,0:T(8,128)(2,1)} %get-tuple-element.57), channel_id=1, source_target_pairs={{0,8},{1,9},{2,10},{3,11},{4,12},{5,13},{6,14},{7,15},{8,0},{9,1},... | collective-permute-start | bytes 786440 | tf_op jit(solution)/shard_map/ppermute | solution.py:290
  281.1 18.1 %transform.9 = (bf16[8,128,256]{2,1,0:T(8,128)(2,1)}, bf16[8,128,256]{2,1,0:T(8,128)(2,1)}, bf16[8,128,256]{2,1,0:T(8,128)(2,1)}, bf16[8,128,256]{2,1,0:T(8,128)(2,1)}) custom-call(s32[1]{0:T(128)} %bitcast.refs_0_, bf16[8,256,2048]{2,1,0:T(8,128)(2,1)} %get-tuple-element.38.refs_1_, bf16[8,256,2048]{2,1,0:T(8,128)(2,1)} %get-tuple-element.40.refs_2_, ...), custom_call_target="tpu_custom_call" | custom-call | tf_op jit(solution)/shard_map/transform/pallas_call | solution.py:341
  299.2 24.9 %collective-permute-start.22 = (bf16[8,128,256]{2,1,0:T(8,128)(2,1)}, bf16[8,128,256]{2,1,0:T(8,128)(2,1)S(1)}, u32[]{:S(2)}, u32[]{:S(2)}) collective-permute-start(bf16[8,128,256]{2,1,0:T(8,128)(2,1)} %get-tuple-element.61), channel_id=1, source_target_pairs={{0,4},{1,5},{2,6},{3,7},{4,0},{5,1},{6,2},{7,3},{8,12},{9,13},{10,... | collective-permute-start | bytes 1572872 | tf_op jit(solution)/shard_map/ppermute | solution.py:290
  334.7 7.8 %collective-permute-done.22 = bf16[8,128,256]{2,1,0:T(8,128)(2,1)S(1)} collective-permute-done((bf16[8,128,256]{2,1,0:T(8,128)(2,1)}, bf16[8,128,256]{2,1,0:T(8,128)(2,1)S(1)}, u32[]{:S(2)}, u32[]{:S(2)}) %collective-permute-start.22) | collective-permute-done | bytes 524320 | tf_op jit(solution)/shard_map/ppermute | solution.py:290
  343.3 21.0 %collective-permute-done.23 = bf16[8,128,256]{2,1,0:T(8,128)(2,1)S(1)} collective-permute-done((bf16[8,128,256]{2,1,0:T(8,128)(2,1)}, bf16[8,128,256]{2,1,0:T(8,128)(2,1)S(1)}, u32[]{:S(2)}, u32[]{:S(2)}) %collective-permute-start.23) | collective-permute-done | bytes 524320 | tf_op jit(solution)/shard_map/ppermute | solution.py:290
  376.4 5.8 collective-permute-start.29
  390.9 23.6 %collective-permute-start.26 = (bf16[8,128,256]{2,1,0:T(8,128)(2,1)S(1)}, bf16[8,128,256]{2,1,0:T(8,128)(2,1)S(1)}, u32[]{:S(2)}, u32[]{:S(2)}) collective-permute-start(bf16[8,128,256]{2,1,0:T(8,128)(2,1)S(1)} %get-tuple-element.78), channel_id=1, source_target_pairs={{0,8},{1,9},{2,10},{3,11},{4,12},{5,13},{6,14},{7,15},{8,0},{9,1},... | collective-permute-start | bytes 1572872 | tf_op jit(solution)/shard_map/ppermute | solution.py:290
  414.5 50.8 %collective-permute-done.29 = bf16[8,128,256]{2,1,0:T(8,128)(2,1)S(1)} collective-permute-done((bf16[8,128,256]{2,1,0:T(8,128)(2,1)S(1)}, bf16[8,128,256]{2,1,0:T(8,128)(2,1)S(1)}, u32[]{:S(2)}, u32[]{:S(2)}) %collective-permute-start.29) | collective-permute-done | bytes 524320 | tf_op jit(solution)/shard_map/ppermute | solution.py:290
  468.8 47.6 %collective-permute-start.7 = (bf16[8,224,256]{2,1,0:T(8,128)(2,1)S(1)}, bf16[8,224,256]{2,1,0:T(8,128)(2,1)}, u32[]{:S(2)}, u32[]{:S(2)}) collective-permute-start(bf16[8,224,256]{2,1,0:T(8,128)(2,1)S(1)} %get-tuple-element.67), channel_id=1, source_target_pairs={{0,4},{1,5},{2,6},{3,7},{4,0},{5,1},{6,2},{7,3},{8,12},{9,13},{10,... | collective-permute-start | bytes 2752520 | tf_op jit(solution)/shard_map/ppermute | solution.py:290
  518.0 9.3 %collective-permute-done.26 = bf16[8,128,256]{2,1,0:T(8,128)(2,1)S(1)} collective-permute-done((bf16[8,128,256]{2,1,0:T(8,128)(2,1)S(1)}, bf16[8,128,256]{2,1,0:T(8,128)(2,1)S(1)}, u32[]{:S(2)}, u32[]{:S(2)}) %collective-permute-start.26) | collective-permute-done | bytes 524320 | tf_op jit(solution)/shard_map/ppermute | solution.py:290
  532.6 6.8 %correlate.6.refs_4_ = f32[2,32,512,512]{3,2,1,0:T(8,128)} custom-call(bf16[8,1,2,64,256]{4,3,2,1,0:T(8,128)(2,1)} %bitcast.85, bf16[8,1,2,64,256]{4,3,2,1,0:T(8,128)(2,1)} %bitcast.90, bf16[8,1,2,64,256]{4,3,2,1,0:T(8,128)(2,1)} %bitcast.89, bf16[8,1,2,64,256]{4,3,2,1,0:T(8,128)(2,1)} %bitcast.88), custom_call_target="tpu_custom_call" | custom-call | tf_op jit(solution)/shard_map/correlate/pallas_call | solution.py:376
  539.4 6.8 %correlate.7.refs_1_ = f32[2,32,512,512]{3,2,1,0:T(8,128)} custom-call(bf16[8,1,2,64,256]{4,3,2,1,0:T(8,128)(2,1)} %bitcast.86, bf16[8,1,2,64,256]{4,3,2,1,0:T(8,128)(2,1)} %bitcast.93, bf16[8,1,2,64,256]{4,3,2,1,0:T(8,128)(2,1)} %bitcast.92, bf16[8,1,2,64,256]{4,3,2,1,0:T(8,128)(2,1)} %bitcast.91, ...), custom_call_target="tpu_custom_call", output_to_operand_aliasing={{}: (4, {})} | custom-call | tf_op jit(solution)/shard_map/correlate/pallas_call | solution.py:376
  546.1 11.2 %correlate.8.refs_1_ = f32[2,32,512,512]{3,2,1,0:T(8,128)} custom-call(bf16[8,12,1,128,256]{4,3,2,1,0:T(8,128)(2,1)} %bitcast.28.refs_0_, f32[2,32,512,512]{3,2,1,0:T(8,128)} %correlate.7.refs_1_), custom_call_target="tpu_custom_call", output_to_operand_aliasing={{}: (1, {})} | custom-call | tf_op jit(solution)/shard_map/correlate/pallas_call | solution.py:376
  557.3 6.6 %correlate.9.refs_4_ = f32[2,32,512,512]{3,2,1,0:T(8,128)} custom-call(bf16[8,12,2,64,256]{4,3,2,1,0:T(8,128)(2,1)} %bitcast.27.refs_0_, f32[2,32,512,512]{3,2,1,0:T(8,128)} %correlate.8.refs_1_), custom_call_target="tpu_custom_call", output_to_operand_aliasing={{}: (1, {})} | custom-call | tf_op jit(solution)/shard_map/correlate/pallas_call | solution.py:376
  563.9 11.2 %collective-permute-done.8 = bf16[8,224,256]{2,1,0:T(8,128)(2,1)} collective-permute-done((bf16[8,224,256]{2,1,0:T(8,128)(2,1)}, bf16[8,224,256]{2,1,0:T(8,128)(2,1)}, u32[]{:S(2)}, u32[]{:S(2)}) %collective-permute-start.8) | collective-permute-done | bytes 917536 | tf_op jit(solution)/shard_map/ppermute | solution.py:290
  575.1 5.5 collective-permute-done.7
  580.6 10.3 %correlate.10.refs_4_ = f32[2,32,512,512]{3,2,1,0:T(8,128)} custom-call(bf16[8,1,2,112,256]{4,3,2,1,0:T(8,128)(2,1)} %bitcast.83, bf16[8,1,2,112,256]{4,3,2,1,0:T(8,128)(2,1)} %bitcast.10.refs_1_, bf16[8,1,2,112,256]{4,3,2,1,0:T(8,128)(2,1)} %bitcast.12.refs_2_, bf16[8,1,2,112,256]{4,3,2,1,0:T(8,128)(2,1)} %bitcast.87, ...), custom_call_target="tpu_custom_call", output_to_operand_aliasing={{}: (4, {})} | custom-call | tf_op jit(solution)/shard_map/correlate/pallas_call | solution.py:376
  591.0 12.3 %collective-permute-done.5 = bf16[8,160,256]{2,1,0:T(8,128)(2,1)} collective-permute-done((bf16[8,160,256]{2,1,0:T(8,128)(2,1)}, bf16[8,160,256]{2,1,0:T(8,128)(2,1)}, u32[]{:S(2)}, u32[]{:S(2)}) %collective-permute-start.5) | collective-permute-done | bytes 655392 | tf_op jit(solution)/shard_map/ppermute | solution.py:290
  608.7 8.0 %correlate.11 = f32[2,32,512,512]{3,2,1,0:T(8,128)} custom-call(bf16[8,1,2,80,256]{4,3,2,1,0:T(8,128)(2,1)} %bitcast.84, bf16[8,1,2,80,256]{4,3,2,1,0:T(8,128)(2,1)} %bitcast.3.refs_1_, bf16[8,1,2,80,256]{4,3,2,1,0:T(8,128)(2,1)} %bitcast.5.refs_2_, bf16[8,1,2,80,256]{4,3,2,1,0:T(8,128)(2,1)} %bitcast.7.refs_3_, ...), custom_call_target="tpu_custom_call", output_to_operand_aliasing={{}: (4, {})} | custom-call | tf_op jit(solution)/shard_map/correlate/pallas_call | solution.py:376
  (101 shorter events, 106.2 us)
Async XLA Ops:
  7.1 41.1 %collective-permute-start.3 = (bf16[128,6144]{1,0:T(8,128)(2,1)}, bf16[128,6144]{1,0:T(8,128)(2,1)S(1)}, u32[]{:S(2)}, u32[]{:S(2)}) collective-permute-start(bf16[128,6144]{1,0:T(8,128)(2,1)} %get-tuple-element.36), channel_id=1, source_target_pairs={{0,1},{1,2},{2,3},{3,4},{4,5},{5,6},{6,7},{7,8},{8,9},{9,10},{10,1... | collective-permute-start | bytes 4718600 | tf_op jit(solution)/shard_map/ppermute | solution.py:23
  9.6 55.2 %collective-permute-start.2 = (bf16[128,6144]{1,0:T(8,128)(2,1)}, bf16[128,6144]{1,0:T(8,128)(2,1)S(1)}, u32[]{:S(2)}, u32[]{:S(2)}) collective-permute-start(bf16[128,6144]{1,0:T(8,128)(2,1)} %get-tuple-element.35), channel_id=1, source_target_pairs={{0,1},{1,2},{2,3},{4,5},{5,6},{6,7},{8,9},{9,10},{10,11},{12,13},{... | collective-permute-start | bytes 4718600 | tf_op jit(solution)/shard_map/ppermute | solution.py:23
  14.2 50.6 %collective-permute-start.1 = (bf16[128,6144]{1,0:T(8,128)(2,1)}, bf16[128,6144]{1,0:T(8,128)(2,1)}, u32[]{:S(2)}, u32[]{:S(2)}) collective-permute-start(bf16[128,6144]{1,0:T(8,128)(2,1)} %collective-permute-done), channel_id=1, source_target_pairs={{6,4},{10,8},{14,12},{22,20},{26,24},{30,28}} | collective-permute-start | bytes 4718600 | tf_op jit(solution)/shard_map/ppermute | solution.py:23
  101.1 41.5 %all-to-all-start = ((bf16[8,4,128,256]{3,2,1,0:T(8,128)(2,1)}), bf16[8,4,128,256]{3,2,1,0:T(8,128)(2,1)S(1)}, u32[]{:S(2)}, u32[]{:S(2)}) async-start(bf16[8,4,128,256]{3,2,1,0:T(8,128)(2,1)} %transform.8), calls=%async_computation | async-start | bytes 4194304 | tf_op jit(solution)/shard_map/all_to_all | solution.py:301
  143.9 30.0 %all-to-all-start.1 = ((bf16[8,4,128,256]{3,2,1,0:T(8,128)(2,1)}), bf16[8,4,128,256]{3,2,1,0:T(8,128)(2,1)S(1)}, u32[]{:S(2)}, u32[]{:S(2)}) async-start(bf16[8,4,128,256]{3,2,1,0:T(8,128)(2,1)} %transform.7), calls=%async_computation.1 | async-start | bytes 4194304 | tf_op jit(solution)/shard_map/all_to_all | solution.py:301
  173.9 47.1 %all-to-all-start.2 = ((bf16[8,4,224,256]{3,2,1,0:T(8,128)(2,1)}), bf16[8,4,224,256]{3,2,1,0:T(8,128)(2,1)}, u32[]{:S(2)}, u32[]{:S(2)}) async-start(bf16[8,4,224,256]{3,2,1,0:T(8,128)(2,1)} %transform.6), calls=%async_computation.2 | async-start | bytes 7340032 | tf_op jit(solution)/shard_map/all_to_all | solution.py:301
  221.0 145.0 %all-to-all-start.3 = ((bf16[8,4,160,256]{3,2,1,0:T(8,128)(2,1)}), bf16[8,4,160,256]{3,2,1,0:T(8,128)(2,1)S(1)}, u32[]{:S(2)}, u32[]{:S(2)}) async-start(bf16[8,4,160,256]{3,2,1,0:T(8,128)(2,1)} %transform.5), calls=%async_computation.3 | async-start | bytes 5242880 | tf_op jit(solution)/shard_map/all_to_all | solution.py:301
  228.3 24.1 %collective-permute-start.12 = (bf16[8,128,128]{2,1,0:T(8,128)(2,1)}, bf16[8,128,128]{2,1,0:T(8,128)(2,1)S(1)}, u32[]{:S(2)}, u32[]{:S(2)}) collective-permute-start(bf16[8,128,128]{2,1,0:T(8,128)(2,1)} %get-tuple-element.48), channel_id=1, source_target_pairs={{0,8},{1,9},{2,10},{3,11},{4,12},{5,13},{6,14},{7,15},{8,0},{9,1},... | collective-permute-start | bytes 786440 | tf_op jit(solution)/shard_map/ppermute | solution.py:290
  231.3 35.5 %collective-permute-start.13 = (bf16[8,128,128]{2,1,0:T(8,128)(2,1)}, bf16[8,128,128]{2,1,0:T(8,128)(2,1)S(1)}, u32[]{:S(2)}, u32[]{:S(2)}) collective-permute-start(bf16[8,128,128]{2,1,0:T(8,128)(2,1)} %get-tuple-element.49), channel_id=1, source_target_pairs={{0,8},{1,9},{2,10},{3,11},{4,12},{5,13},{6,14},{7,15},{8,0},{9,1},... | collective-permute-start | bytes 786440 | tf_op jit(solution)/shard_map/ppermute | solution.py:290
  231.3 36.4 %collective-permute-start.14 = (bf16[8,128,128]{2,1,0:T(8,128)(2,1)}, bf16[8,128,128]{2,1,0:T(8,128)(2,1)S(1)}, u32[]{:S(2)}, u32[]{:S(2)}) collective-permute-start(bf16[8,128,128]{2,1,0:T(8,128)(2,1)} %get-tuple-element.50), channel_id=1, source_target_pairs={{0,12},{1,13},{2,14},{3,15},{4,8},{5,9},{6,10},{7,11},{8,4},{9,5},... | collective-permute-start | bytes 786440 | tf_op jit(solution)/shard_map/ppermute | solution.py:290
  246.3 29.2 %collective-permute-start.15 = (bf16[8,128,128]{2,1,0:T(8,128)(2,1)}, bf16[8,128,128]{2,1,0:T(8,128)(2,1)S(1)}, u32[]{:S(2)}, u32[]{:S(2)}) collective-permute-start(bf16[8,128,128]{2,1,0:T(8,128)(2,1)} %get-tuple-element.51), channel_id=1, source_target_pairs={{0,12},{1,13},{2,14},{3,15},{4,8},{5,9},{6,10},{7,11},{8,4},{9,5},... | collective-permute-start | bytes 786440 | tf_op jit(solution)/shard_map/ppermute | solution.py:290
  251.6 25.3 %collective-permute-start.16 = (bf16[8,128,128]{2,1,0:T(8,128)(2,1)}, bf16[8,128,128]{2,1,0:T(8,128)(2,1)S(1)}, u32[]{:S(2)}, u32[]{:S(2)}) collective-permute-start(bf16[8,128,128]{2,1,0:T(8,128)(2,1)} %get-tuple-element.54), channel_id=1, source_target_pairs={{0,4},{1,5},{2,6},{3,7},{4,0},{5,1},{6,2},{7,3},{8,12},{9,13},{10,... | collective-permute-start | bytes 786440 | tf_op jit(solution)/shard_map/ppermute | solution.py:290
  252.5 46.7 %collective-permute-start.17 = (bf16[8,128,128]{2,1,0:T(8,128)(2,1)}, bf16[8,128,128]{2,1,0:T(8,128)(2,1)}, u32[]{:S(2)}, u32[]{:S(2)}) collective-permute-start(bf16[8,128,128]{2,1,0:T(8,128)(2,1)} %get-tuple-element.55), channel_id=1, source_target_pairs={{0,4},{1,5},{2,6},{3,7},{4,0},{5,1},{6,2},{7,3},{8,12},{9,13},{10,... | collective-permute-start | bytes 786440 | tf_op jit(solution)/shard_map/ppermute | solution.py:290
  267.7 58.2 %collective-permute-start.18 = (bf16[8,128,128]{2,1,0:T(8,128)(2,1)}, bf16[8,128,128]{2,1,0:T(8,128)(2,1)}, u32[]{:S(2)}, u32[]{:S(2)}) collective-permute-start(bf16[8,128,128]{2,1,0:T(8,128)(2,1)} %get-tuple-element.56), channel_id=1, source_target_pairs={{0,8},{1,9},{2,10},{3,11},{4,12},{5,13},{6,14},{7,15},{8,0},{9,1},... | collective-permute-start | bytes 786440 | tf_op jit(solution)/shard_map/ppermute | solution.py:290
  267.7 59.7 %collective-permute-start.19 = (bf16[8,128,128]{2,1,0:T(8,128)(2,1)}, bf16[8,128,128]{2,1,0:T(8,128)(2,1)}, u32[]{:S(2)}, u32[]{:S(2)}) collective-permute-start(bf16[8,128,128]{2,1,0:T(8,128)(2,1)} %get-tuple-element.57), channel_id=1, source_target_pairs={{0,8},{1,9},{2,10},{3,11},{4,12},{5,13},{6,14},{7,15},{8,0},{9,1},... | collective-permute-start | bytes 786440 | tf_op jit(solution)/shard_map/ppermute | solution.py:290
  276.4 54.5 %collective-permute-start.20 = (bf16[8,128,128]{2,1,0:T(8,128)(2,1)}, bf16[8,128,128]{2,1,0:T(8,128)(2,1)}, u32[]{:S(2)}, u32[]{:S(2)}) collective-permute-start(bf16[8,128,128]{2,1,0:T(8,128)(2,1)} %get-tuple-element.58), channel_id=1, source_target_pairs={{0,12},{1,13},{2,14},{3,15},{4,8},{5,9},{6,10},{7,11},{8,4},{9,5},... | collective-permute-start | bytes 786440 | tf_op jit(solution)/shard_map/ppermute | solution.py:290
  276.9 53.9 %collective-permute-start.21 = (bf16[8,128,128]{2,1,0:T(8,128)(2,1)}, bf16[8,128,128]{2,1,0:T(8,128)(2,1)}, u32[]{:S(2)}, u32[]{:S(2)}) collective-permute-start(bf16[8,128,128]{2,1,0:T(8,128)(2,1)} %get-tuple-element.59), channel_id=1, source_target_pairs={{0,12},{1,13},{2,14},{3,15},{4,8},{5,9},{6,10},{7,11},{8,4},{9,5},... | collective-permute-start | bytes 786440 | tf_op jit(solution)/shard_map/ppermute | solution.py:290
  299.2 43.2 %collective-permute-start.22 = (bf16[8,128,256]{2,1,0:T(8,128)(2,1)}, bf16[8,128,256]{2,1,0:T(8,128)(2,1)S(1)}, u32[]{:S(2)}, u32[]{:S(2)}) collective-permute-start(bf16[8,128,256]{2,1,0:T(8,128)(2,1)} %get-tuple-element.61), channel_id=1, source_target_pairs={{0,4},{1,5},{2,6},{3,7},{4,0},{5,1},{6,2},{7,3},{8,12},{9,13},{10,... | collective-permute-start | bytes 1572872 | tf_op jit(solution)/shard_map/ppermute | solution.py:290
  325.9 38.4 %collective-permute-start.23 = (bf16[8,128,256]{2,1,0:T(8,128)(2,1)}, bf16[8,128,256]{2,1,0:T(8,128)(2,1)S(1)}, u32[]{:S(2)}, u32[]{:S(2)}) collective-permute-start(bf16[8,128,256]{2,1,0:T(8,128)(2,1)} %get-tuple-element.62), channel_id=1, source_target_pairs={{0,8},{1,9},{2,10},{3,11},{4,12},{5,13},{6,14},{7,15},{8,0},{9,1},... | collective-permute-start | bytes 1572872 | tf_op jit(solution)/shard_map/ppermute | solution.py:290
  327.4 37.8 %collective-permute-start.24 = (bf16[8,128,256]{2,1,0:T(8,128)(2,1)}, bf16[8,128,256]{2,1,0:T(8,128)(2,1)S(1)}, u32[]{:S(2)}, u32[]{:S(2)}) collective-permute-start(bf16[8,128,256]{2,1,0:T(8,128)(2,1)} %get-tuple-element.63), channel_id=1, source_target_pairs={{0,12},{1,13},{2,14},{3,15},{4,8},{5,9},{6,10},{7,11},{8,4},{9,5},... | collective-permute-start | bytes 1572872 | tf_op jit(solution)/shard_map/ppermute | solution.py:290
  366.0 180.1 %all-to-all-start.4 = ((bf16[8,12,128,256]{3,2,1,0:T(8,128)(2,1)}), bf16[8,12,128,256]{3,2,1,0:T(8,128)(2,1)}, u32[]{:S(2)}, u32[]{:S(2)}) async-start(bf16[8,12,128,256]{3,2,1,0:T(8,128)(2,1)} %bitcast_dynamic-update-slice_fusion), calls=%async_computation.4 | async-start | bytes 12582912 | tf_op jit(solution)/shard_map/all_to_all | solution.py:301
  376.4 89.0 %collective-permute-start.29 = (bf16[8,128,256]{2,1,0:T(8,128)(2,1)S(1)}, bf16[8,128,256]{2,1,0:T(8,128)(2,1)S(1)}, u32[]{:S(2)}, u32[]{:S(2)}) collective-permute-start(bf16[8,128,256]{2,1,0:T(8,128)(2,1)S(1)} %get-tuple-element.74), channel_id=1, source_target_pairs={{0,8},{1,9},{2,10},{3,11},{4,12},{5,13},{6,14},{7,15},{8,0},{9,1},... | collective-permute-start | bytes 1572872 | tf_op jit(solution)/shard_map/ppermute | solution.py:290
  382.2 83.2 %collective-permute-start.28 = (bf16[8,128,256]{2,1,0:T(8,128)(2,1)S(1)}, bf16[8,128,256]{2,1,0:T(8,128)(2,1)S(1)}, u32[]{:S(2)}, u32[]{:S(2)}) collective-permute-start(bf16[8,128,256]{2,1,0:T(8,128)(2,1)S(1)} %get-tuple-element.75), channel_id=1, source_target_pairs={{0,4},{1,5},{2,6},{3,7},{4,0},{5,1},{6,2},{7,3},{8,12},{9,13},{10,... | collective-permute-start | bytes 1572872 | tf_op jit(solution)/shard_map/ppermute | solution.py:290
  386.1 144.0 %collective-permute-start.9 = (bf16[8,224,256]{2,1,0:T(8,128)(2,1)S(1)}, bf16[8,224,256]{2,1,0:T(8,128)(2,1)S(1)}, u32[]{:S(2)}, u32[]{:S(2)}) collective-permute-start(bf16[8,224,256]{2,1,0:T(8,128)(2,1)S(1)} %get-tuple-element.65), channel_id=1, source_target_pairs={{0,12},{1,13},{2,14},{3,15},{4,8},{5,9},{6,10},{7,11},{8,4},{9,5},... | collective-permute-start | bytes 2752520 | tf_op jit(solution)/shard_map/ppermute | solution.py:290
  389.4 79.4 %collective-permute-start.27 = (bf16[8,128,256]{2,1,0:T(8,128)(2,1)S(1)}, bf16[8,128,256]{2,1,0:T(8,128)(2,1)S(1)}, u32[]{:S(2)}, u32[]{:S(2)}) collective-permute-start(bf16[8,128,256]{2,1,0:T(8,128)(2,1)S(1)} %get-tuple-element.77), channel_id=1, source_target_pairs={{0,12},{1,13},{2,14},{3,15},{4,8},{5,9},{6,10},{7,11},{8,4},{9,5},... | collective-permute-start | bytes 1572872 | tf_op jit(solution)/shard_map/ppermute | solution.py:290
  390.9 136.3 %collective-permute-start.26 = (bf16[8,128,256]{2,1,0:T(8,128)(2,1)S(1)}, bf16[8,128,256]{2,1,0:T(8,128)(2,1)S(1)}, u32[]{:S(2)}, u32[]{:S(2)}) collective-permute-start(bf16[8,128,256]{2,1,0:T(8,128)(2,1)S(1)} %get-tuple-element.78), channel_id=1, source_target_pairs={{0,8},{1,9},{2,10},{3,11},{4,12},{5,13},{6,14},{7,15},{8,0},{9,1},... | collective-permute-start | bytes 1572872 | tf_op jit(solution)/shard_map/ppermute | solution.py:290
  465.3 64.8 %collective-permute-start.25 = (bf16[8,128,256]{2,1,0:T(8,128)(2,1)S(1)}, bf16[8,128,256]{2,1,0:T(8,128)(2,1)S(1)}, u32[]{:S(2)}, u32[]{:S(2)}) collective-permute-start(bf16[8,128,256]{2,1,0:T(8,128)(2,1)S(1)} %get-tuple-element.79), channel_id=1, source_target_pairs={{0,4},{1,5},{2,6},{3,7},{4,0},{5,1},{6,2},{7,3},{8,12},{9,13},{10,... | collective-permute-start | bytes 1572872 | tf_op jit(solution)/shard_map/ppermute | solution.py:290
  465.4 109.6 %collective-permute-start.8 = (bf16[8,224,256]{2,1,0:T(8,128)(2,1)}, bf16[8,224,256]{2,1,0:T(8,128)(2,1)}, u32[]{:S(2)}, u32[]{:S(2)}) collective-permute-start(bf16[8,224,256]{2,1,0:T(8,128)(2,1)} %get-tuple-element.66), channel_id=1, source_target_pairs={{0,8},{1,9},{2,10},{3,11},{4,12},{5,13},{6,14},{7,15},{8,0},{9,1},... | collective-permute-start | bytes 2752520 | tf_op jit(solution)/shard_map/ppermute | solution.py:290
  468.8 111.8 %collective-permute-start.7 = (bf16[8,224,256]{2,1,0:T(8,128)(2,1)S(1)}, bf16[8,224,256]{2,1,0:T(8,128)(2,1)}, u32[]{:S(2)}, u32[]{:S(2)}) collective-permute-start(bf16[8,224,256]{2,1,0:T(8,128)(2,1)S(1)} %get-tuple-element.67), channel_id=1, source_target_pairs={{0,4},{1,5},{2,6},{3,7},{4,0},{5,1},{6,2},{7,3},{8,12},{9,13},{10,... | collective-permute-start | bytes 2752520 | tf_op jit(solution)/shard_map/ppermute | solution.py:290
  527.2 63.7 %collective-permute-start.6 = (bf16[8,160,256]{2,1,0:T(8,128)(2,1)}, bf16[8,160,256]{2,1,0:T(8,128)(2,1)}, u32[]{:S(2)}, u32[]{:S(2)}) collective-permute-start(bf16[8,160,256]{2,1,0:T(8,128)(2,1)} %get-tuple-element.69), channel_id=1, source_target_pairs={{0,12},{1,13},{2,14},{3,15},{4,8},{5,9},{6,10},{7,11},{8,4},{9,5},... | collective-permute-start | bytes 1966088 | tf_op jit(solution)/shard_map/ppermute | solution.py:290
  530.2 73.1 %collective-permute-start.5 = (bf16[8,160,256]{2,1,0:T(8,128)(2,1)}, bf16[8,160,256]{2,1,0:T(8,128)(2,1)}, u32[]{:S(2)}, u32[]{:S(2)}) collective-permute-start(bf16[8,160,256]{2,1,0:T(8,128)(2,1)} %get-tuple-element.70), channel_id=1, source_target_pairs={{0,8},{1,9},{2,10},{3,11},{4,12},{5,13},{6,14},{7,15},{8,0},{9,1},... | collective-permute-start | bytes 1966088 | tf_op jit(solution)/shard_map/ppermute | solution.py:290
  531.1 77.5 %collective-permute-start.4 = (bf16[8,160,256]{2,1,0:T(8,128)(2,1)}, bf16[8,160,256]{2,1,0:T(8,128)(2,1)}, u32[]{:S(2)}, u32[]{:S(2)}) collective-permute-start(bf16[8,160,256]{2,1,0:T(8,128)(2,1)} %get-tuple-element.71), channel_id=1, source_target_pairs={{0,4},{1,5},{2,6},{3,7},{4,0},{5,1},{6,2},{7,3},{8,12},{9,13},{10,... | collective-permute-start | bytes 1966088 | tf_op jit(solution)/shard_map/ppermute | solution.py:290
  (18 other events, 696.3 us)
